TPU v7x, 32 devices: a whole 2x2x4 slice. The times are simulated.
32 devices in a mesh: rad: 4 (over z), ma: 8 (over y, x, core).
Axes of the slice: x: 2, y: 2, z: 4, core: 2. Of those that a mesh axis runs over, the one named last changes fastest.
Arguments:
- spectrum: bfloat16 [4, 512, 512, 384], P(None, 'ma', 'rad'), may hold values from -6 to 6
- radial_table: bfloat16 [12, 384], replicated, may hold values from -0.3125 to 0.3125
- legendre: bfloat16 [512, 512, 512], P('ma', 'rad'), may hold values from -0.375 to 0.375
- order_table: int32 [512], replicated, may hold values from 0 to 511, each once
- cylinder_row: int32 [512, 12], P(('rad', 'ma')), may hold values from 0 to 127
- column_weight: float32 [512, 12], P(('rad', 'ma')), may hold values from 0.5 to 2
Outputs:
- column_buoyancy: float32 [128, 1024], P('ma', 'rad')
- advected: float32 [2, 512, 12, 1024], P(None, ('rad', 'ma'))
Inputs may be any that keep to these rules, and one draw needn't show every extreme that they name: `order_table`: each order appears in exactly one slot.
All inputs are finite; a program needn't handle non-finite values.
Results may differ from a plain program's by a relative error of at most 0.008.
Values may be sent and summed in bfloat16 or wider, within the bound.
A program may use at most 128 MiB of HBM per device.

v0:
```python
import math

import jax
import jax.numpy as jnp
from jax import lax
from jax.sharding import PartitionSpec as P

L = 512
NPHI = 1024
QROWS = 16


time_step = 0.05
composition_weight = 0.8


def padded(block, sides, width, periodic):
    for axis, dim in sides:
        count = lax.axis_size(axis)
        forward = [(i, i + 1) for i in range(count - 1)]
        if periodic:
            forward.append((count - 1, 0))
        backward = [(target, source) for source, target in forward]
        low = lax.ppermute(
            lax.slice_in_dim(block, block.shape[dim] - width, None, axis=dim), axis, forward
        )
        high = lax.ppermute(lax.slice_in_dim(block, 0, width, axis=dim), axis, backward)
        block = jnp.concatenate([low, block, high], axis=dim)
    return block


def synthesis_tables(order_table):
    longitude = jnp.arange(NPHI, dtype=jnp.int32)
    phase_index = order_table[:, None] * longitude[None, :] % NPHI
    angles = phase_index.astype(jnp.float32) * (2.0 * math.pi / NPHI)
    weights = jnp.where(order_table == 0, 1.0, 2.0).astype(jnp.float32) / math.sqrt(L)
    cosine = jnp.cos(angles) * weights[:, None]
    sine = jnp.sin(angles) * weights[:, None]
    slopes = (order_table.astype(jnp.float32) / L)[:, None]
    values = jnp.stack([cosine, -sine])
    turned = jnp.stack([-sine * slopes, -cosine * slopes])
    return jnp.concatenate([values, turned], axis=2).astype(jnp.bfloat16)


def stream_velocity(outward_diff, around_diff, radius):
    outward = outward_diff / (2.0 * radius[:, None])
    beside_all = -around_diff * 0.5
    return jnp.stack([outward, beside_all]).astype(jnp.bfloat16)


def owner_velocity(owned, row_block, total_rows):
    lon_padded = padded(owned, (("rad", 1),), 1, True)
    row_padded = padded(owned, (("ma", 0),), 1, False)
    row_index = lax.axis_index("ma") * row_block + jnp.arange(row_block, dtype=jnp.int32)
    radius = 0.35 + 0.65 * (row_index.astype(jnp.float32) + 0.5) / total_rows
    local_velocity = stream_velocity(
        lon_padded[:, 2:] - lon_padded[:, :-2], row_padded[2:] - row_padded[:-2], radius
    )
    velocity = lax.all_gather(local_velocity, "rad", axis=2, tiled=True)
    return lax.all_gather(velocity, "ma", axis=1, tiled=True)


def on_device(spectrum, radial_table, legendre, order_table, cylinder_row, column_weight):
    slot_count = spectrum.shape[1]
    degree_count = spectrum.shape[2]
    level_count = radial_table.shape[0]
    latitude_count = legendre.shape[2]
    rad_count = lax.axis_size("rad")
    ma_count = lax.axis_size("ma")
    total_rows = QROWS * ma_count
    row_block = QROWS
    my_orders = lax.dynamic_slice_in_dim(order_table, lax.axis_index("ma") * slot_count, slot_count)
    my_degrees = lax.axis_index("rad") * degree_count + jnp.arange(degree_count, dtype=jnp.int32)
    allowed = my_degrees[None, :] >= my_orders[:, None]
    masked_table = jnp.where(allowed[:, :, None], legendre, jnp.zeros_like(legendre))
    levels = jnp.einsum(
        "rn,ckln->rckl", radial_table, spectrum, preferred_element_type=jnp.float32
    ).astype(jnp.bfloat16)
    contribution = jnp.einsum(
        "klt,rckl->trck", masked_table, levels, preferred_element_type=jnp.float32
    )
    latitudes = lax.psum_scatter(
        contribution.reshape(
            latitude_count // rad_count * lax.axis_size("rad"), level_count * 4 * slot_count
        ),
        "rad",
        scatter_dimension=0,
        tiled=True,
    ).astype(jnp.bfloat16)
    received = lax.all_to_all(latitudes, "ma", split_axis=0, concat_axis=1, tiled=True)
    lat_rows = received.shape[0]
    coefficients = received.reshape(lat_rows, ma_count, level_count, 2, 2, slot_count)
    tables = synthesis_tables(order_table).reshape(2, ma_count, slot_count, 2 * NPHI)
    synthesis = jnp.einsum(
        "tsrfik,iskq->ftrq", coefficients, tables, preferred_element_type=jnp.float32
    ).astype(jnp.bfloat16)
    fields = synthesis[..., :NPHI].astype(jnp.float32)
    slope_field = synthesis[..., NPHI:].astype(jnp.float32)
    buoyancy = fields[0] - composition_weight * fields[1]
    weighted = (column_weight[:, :, None] * buoyancy).reshape(-1, NPHI)
    point_rows = cylinder_row.reshape(-1)
    row_ids = jnp.arange(total_rows, dtype=jnp.int32)
    selector = (row_ids[:, None] == point_rows[None, :]).astype(jnp.float32)
    partial_value = jnp.dot(
        selector, weighted, precision=lax.Precision.HIGHEST, preferred_element_type=jnp.float32
    )
    owned = lax.psum_scatter(partial_value, "ma", scatter_dimension=0, tiled=True)
    owned = lax.psum_scatter(owned, "rad", scatter_dimension=1, tiled=True)
    velocity = owner_velocity(owned, row_block, total_rows)
    chooser = (point_rows[:, None] == row_ids[None, :]).astype(jnp.bfloat16)
    moved = jnp.einsum("pj,cjq->cpq", chooser, velocity, preferred_element_type=jnp.float32)
    moved = moved.reshape(2, lat_rows, level_count, NPHI)
    inverse = 1.0 / (0.35 + 0.65 * (cylinder_row.astype(jnp.float32) + 0.5) / total_rows)
    advected = fields - time_step * inverse[None, :, :, None] * (
        moved[1][None] * slope_field + moved[0][None] * fields
    )
    return (owned, advected)


def solution(mesh):
    return jax.shard_map(
        on_device,
        mesh=mesh,
        in_specs=(
            P(None, "ma", "rad", None),
            P(),
            P("ma", "rad", None),
            P(),
            P(("rad", "ma"), None),
            P(("rad", "ma"), None),
        ),
        out_specs=(P("ma", "rad"), P(None, ("rad", "ma"), None, None)),
        check_vma=False,
    )
```

profile of v0, /device:TPU:1, one launch (start us, length us, event | category | flops | bytes accessed | tf_op | source)
XLA Modules:
  0.0 280.5 jit_solution(5860157621208165237)
XLA Ops:
  7.2 0.0 copy-start
  7.2 0.0 reduce-scatter.4.cloned.1.call-start
  7.2 0.8 dynamic_slice.3
  8.0 0.1 broadcast_compare_fusion
  8.1 0.0 copy-done
  8.1 17.6 %fusion.14 = f32[512,12,4,64]{0,1,2,3:T(8,128)} fusion(bf16[64,128,512]{2,1,0:T(8,128)(2,1)} %param.8, pred[64,128]{1,0:T(8,128)(4,1)S(1)} %broadcast_compare_fusion, bf16[4,64,128,384]{3,2,1,0:T(8,128)(2,1)} %param.6, bf16[12,384]{1,0:T(8,128)(2,1)S(1)} %copy-done), kind=kOutput, calls=%fused_computation.15 | convolution fusion | flops 709230592 | bytes 39863296 | tf_op jit(solution)/shard_map/klt,rckl->trck/dot_general | solution.py:79
  25.6 9.7 %copy.21 = f32[512,12,4,64]{0,3,2,1:T(8,128)} copy(f32[512,12,4,64]{0,1,2,3:T(8,128)} %fusion.14) | data formatting | bytes 12582912 | tf_op jit(solution)/shard_map/klt,rckl->trck/transpose | solution.py:79
  35.4 0.0 reduce-scatter.4.cloned.1.call-update
  35.4 112.9 %reduce-scatter.4.cloned.1.call-done = f32[128,3072]{0,1:T(8,128)} async-done(((f32[512,3072]{0,1:T(8,128)}), f32[128,3072]{0,1:T(8,128)}) %reduce-scatter.4.cloned.1.call-update) | async-done | bytes 1572880 | tf_op jit(solution)/shard_map/reduce_scatter | solution.py:82
  148.3 1.5 convert_element_type.65
  149.8 0.0 copy-start.3
  149.8 0.0 copy-start.2
  149.9 0.0 copy-start.4
  149.9 1.2 copy.22
  151.1 4.4 %all-to-all-start = ((bf16[8,16,3072]{2,1,0:T(8,128)(2,1)}), bf16[8,16,3072]{2,1,0:T(8,128)(2,1)S(1)}, u32[]{:S(2)}, u32[]{:S(2)}) async-start(bf16[8,16,3072]{2,1,0:T(8,128)(2,1)} %bitcast.7), calls=%async_computation.1 | async-start | bytes 1572864 | tf_op jit(solution)/shard_map/all_to_all | solution.py:90
  155.4 0.0 reduce-scatter.6.cloned.1.call-start
  155.4 0.0 copy-done.3
  155.4 0.1 mul.224
  155.5 0.1 mul.230
  155.6 0.1 mul.234
  155.7 0.0 copy-done.2
  155.7 0.1 eq.37
  155.8 0.0 copy-done.4
  155.8 0.1 mul.222
  155.9 11.5 %fusion.24 = (bf16[1,8,64,1024]{3,2,1,0:T(8,128)(2,1)}, bf16[1,8,64,1024]{3,2,1,0:T(8,128)(2,1)}, bf16[1,8,64,1024]{3,2,1,0:T(8,128)(2,1)}, bf16[1,8,64,1024]{3,2,1,0:T(8,128)(2,1)}) fusion(f32[8,64]{1,0:T(8,128)S(1)} %mul.230, s32[8,64]{1,0:T(8,128)S(1)} %mul.224, f32[8,64]{1,0:T(8,128)S(1)} %mul.234), kind=kLoop, calls=%fused_computation.31 | loop fusion | flops 12582912 | bytes 4200448 | tf_op jit(solution)/shard_map/convert.8
  167.4 0.0 all-to-all-done
  167.4 1.0 reshape.293
  168.4 4.5 %fusion.17 = bf16[2,16,12,2048]{3,1,0,2:T(8,128)(2,1)S(1)} fusion(bf16[1,8,64,1024]{3,2,1,0:T(8,128)(2,1)} %get-tuple-element.20, bf16[1,8,64,1024]{3,2,1,0:T(8,128)(2,1)} %get-tuple-element.21, bf16[1,8,64,1024]{3,2,1,0:T(8,128)(2,1)} %get-tuple-element.19, bf16[1,8,64,1024]{3,2,1,0:T(8,128)(2,1)} %get-tuple-element.18, ...), kind=kOutput, calls=%fused_computation.20 | convolution fusion | flops 1628176384 | bytes 6553600 | tf_op jit(solution)/shard_map/tsrfik,iskq->ftrq/dot_general | solution.py:94
  172.9 0.2 slice_convert_fusion
  173.1 0.1 fusion.30
  173.2 0.5 copy.25
  173.7 0.1 sub.17
  173.8 1.4 fusion.31
  175.1 0.0 reduce-scatter.6.cloned.1.call-update
  175.2 0.0 reduce-scatter.8.cloned.1.call-start
  175.2 34.1 %reduce-scatter.6.cloned.1.call-done = f32[16,1024]{1,0:T(8,128)} async-done(((f32[128,1024]{1,0:T(8,128)}), f32[16,1024]{1,0:T(8,128)}) %reduce-scatter.6.cloned.1.call-update) | async-done | bytes 65552 | tf_op jit(solution)/shard_map/reduce_scatter | solution.py:107
  209.3 0.0 reduce-scatter.8.cloned.1.call-update
  209.4 0.1 copy.26
  209.4 20.2 %reduce-scatter.8.cloned.1.call-done = f32[16,256]{1,0:T(8,128)} async-done(((f32[16,1024]{1,0:T(8,128)}), f32[16,256]{1,0:T(8,128)}) %reduce-scatter.8.cloned.1.call-update) | async-done | bytes 16400 | tf_op jit(solution)/shard_map/reduce_scatter | solution.py:108
  229.7 0.7 fusion.55
  230.4 4.9 %collective-permute-start.2 = (f32[1,256]{1,0:T(1,128)S(1)}, f32[1,256]{1,0:T(1,128)S(1)}, u32[]{:S(2)}, u32[]{:S(2)}) collective-permute-start(f32[1,256]{1,0:T(1,128)S(1)} %get-tuple-element.14), channel_id=1, source_target_pairs={{1,0},{2,1},{3,2},{4,3},{5,4},{6,5},{7,6},{9,8},{10,9},{11,10},{12... | collective-permute-start | bytes 3080 | tf_op jit(solution)/shard_map/ppermute | solution.py:27
  235.3 3.0 %collective-permute-start.3 = (f32[1,256]{1,0:T(1,128)S(1)}, f32[1,256]{1,0:T(1,128)S(1)}, u32[]{:S(2)}, u32[]{:S(2)}) collective-permute-start(f32[1,256]{1,0:T(1,128)S(1)} %get-tuple-element.15), channel_id=1, source_target_pairs={{0,1},{1,2},{2,3},{3,4},{4,5},{5,6},{6,7},{8,9},{9,10},{10,11},{11... | collective-permute-start | bytes 3080 | tf_op jit(solution)/shard_map/ppermute | solution.py:24
  238.3 0.8 fusion.54
  239.1 0.2 collective-permute-start
  239.3 1.3 collective-permute-start.1
  240.6 1.2 collective-permute-done
  241.8 1.8 collective-permute-done.1
  243.6 0.0 collective-permute-done.2
  243.6 0.0 collective-permute-done.3
  243.6 1.0 fusion.50
  244.6 10.2 %all_gather.6 = bf16[2,16,1024]{2,1,0:T(8,128)(2,1)S(1)} all-gather(bf16[2,16,256]{2,1,0:T(8,128)(2,1)S(1)} %pad_maximum_fusion.4), channel_id=1, replica_groups=mesh['rad'=4,'ma'=8] {'rad'}, dimensions={2}, use_global_device_ids=true | all-gather | bytes 81920 | tf_op jit(solution)/shard_map/all_gather | solution.py:59
  254.8 13.6 %all_gather.7 = bf16[2,128,1024]{2,1,0:T(8,128)(2,1)S(1)} all-gather(bf16[2,16,1024]{2,1,0:T(8,128)(2,1)S(1)} %all_gather.6), channel_id=1, replica_groups=mesh['rad'=4,'ma'=8] {'ma'}, dimensions={1}, use_global_device_ids=true | all-gather | bytes 589824 | tf_op jit(solution)/shard_map/all_gather | solution.py:60
  268.5 0.4 convolution_bitcast_fusion
  268.9 1.0 fusion.53
  269.9 0.1 mul.250
  270.0 0.5 copy.27
  270.5 1.2 mul.253
  271.7 0.5 copy.28
  272.2 0.0 copy-start.1
  272.2 0.5 multiply_subtract_fusion
  272.7 1.2 copy.29
  274.0 0.0 copy-done.1
  (5 shorter events, 0.0 us)
Async XLA Ops:
  7.2 0.9 copy-start
  7.2 141.2 %reduce-scatter.4.cloned.1.call-start = ((), (), s32[]{:S(2)}) async-start(), calls=%async_computation.4 | async-start | bytes 7864320 | tf_op jit(solution)/shard_map/reduce_scatter | solution.py:82
  149.8 5.6 %copy-start.3 = (s32[512]{0:T(512)S(1)}, s32[512]{0:T(512)}, u32[]{:S(2)}) copy-start(s32[512]{0:T(512)} %param.9) | copy-start | bytes 6148
  149.8 5.8 %copy-start.2 = (s32[16,12]{1,0:T(8,128)S(1)}, s32[16,12]{1,0:T(8,128)}, u32[]{:S(2)}) copy-start(s32[16,12]{1,0:T(8,128)} %param.10) | copy-start | bytes 2308
  149.9 5.9 %copy-start.4 = (f32[16,12]{1,0:T(8,128)S(1)}, f32[16,12]{1,0:T(8,128)}, u32[]{:S(2)}) copy-start(f32[16,12]{1,0:T(8,128)} %param.11) | copy-start | bytes 2308
  151.1 16.3 %all-to-all-start = ((bf16[8,16,3072]{2,1,0:T(8,128)(2,1)}), bf16[8,16,3072]{2,1,0:T(8,128)(2,1)S(1)}, u32[]{:S(2)}, u32[]{:S(2)}) async-start(bf16[8,16,3072]{2,1,0:T(8,128)(2,1)} %bitcast.7), calls=%async_computation.1 | async-start | bytes 1572864 | tf_op jit(solution)/shard_map/all_to_all | solution.py:90
  155.4 53.9 %reduce-scatter.6.cloned.1.call-start = ((), (), s32[]{:S(2)}) async-start(), calls=%async_computation.5 | async-start | bytes 589824 | tf_op jit(solution)/shard_map/reduce_scatter | solution.py:107
  175.2 54.5 %reduce-scatter.8.cloned.1.call-start = ((), (), s32[]{:S(2)}) async-start(), calls=%async_computation.6 | async-start | bytes 81920 | tf_op jit(solution)/shard_map/reduce_scatter | solution.py:108
  230.4 13.2 %collective-permute-start.2 = (f32[1,256]{1,0:T(1,128)S(1)}, f32[1,256]{1,0:T(1,128)S(1)}, u32[]{:S(2)}, u32[]{:S(2)}) collective-permute-start(f32[1,256]{1,0:T(1,128)S(1)} %get-tuple-element.14), channel_id=1, source_target_pairs={{1,0},{2,1},{3,2},{4,3},{5,4},{6,5},{7,6},{9,8},{10,9},{11,10},{12... | collective-permute-start | bytes 3080 | tf_op jit(solution)/shard_map/ppermute | solution.py:27
  235.3 8.3 %collective-permute-start.3 = (f32[1,256]{1,0:T(1,128)S(1)}, f32[1,256]{1,0:T(1,128)S(1)}, u32[]{:S(2)}, u32[]{:S(2)}) collective-permute-start(f32[1,256]{1,0:T(1,128)S(1)} %get-tuple-element.15), channel_id=1, source_target_pairs={{0,1},{1,2},{2,3},{3,4},{4,5},{5,6},{6,7},{8,9},{9,10},{10,11},{11... | collective-permute-start | bytes 3080 | tf_op jit(solution)/shard_map/ppermute | solution.py:24
  239.1 2.7 collective-permute-start
  239.3 4.3 %collective-permute-start.1 = (f32[16,1]{1,0:T(8,128)S(1)}, f32[16,1]{1,0:T(8,128)S(1)}, u32[]{:S(2)}, u32[]{:S(2)}) collective-permute-start(f32[16,1]{1,0:T(8,128)S(1)} %get-tuple-element.13), channel_id=1, source_target_pairs={{0,8},{8,16},{16,24},{24,0},{1,9},{9,17},{17,25},{25,1},{2,10},{10... | collective-permute-start | bytes 200 | tf_op jit(solution)/shard_map/ppermute | solution.py:24
  272.2 1.8 copy-start.1
Sparse Core Ops, SparseCore 0:
  35.5 112.7 reduce-scatter.3
  175.3 33.9 reduce-scatter.5
  212.1 17.4 reduce-scatter.7
where the time goes:
time: 281 us
  waiting for transfers between devices  170 us (60%)
  blocking collectives  23.9 us (9%)
  matrix products  23.8 us (8%)
  local copies, waits for them, and re-layouts  19.8 us (7%)
  other arithmetic  14.9 us (5%)
  between operations  13.9 us (5%)
  starting transfers between devices  13.8 us (5%)
    reduce_scatter x1, waiting for transfers between devices, on_device(): lax.psum_scatter(contribution.reshape(latitude_count // rad_count * lax.a...  113 us
    reduce_scatter x1, waiting for transfers between devices, on_device(): lax.psum_scatter(partial_value, 'ma', scatter_dimension=0, tiled=True)  34.1 us
    reduce_scatter x1, waiting for transfers between devices, on_device(): owned = lax.psum_scatter(owned, 'rad', scatter_dimension=1, tiled=True)  20.2 us
    dot_general x1, matrix products, on_device(): jnp.einsum('klt,rckl->trck', masked_table, levels, preferred_element_type...  17.6 us
    all_gather x1, blocking collectives, owner_velocity(): return lax.all_gather(velocity, 'ma', axis=1, tiled=True)  13.6 us
    another operation x1, other arithmetic  11.5 us
    all_gather x1, blocking collectives, owner_velocity(): velocity = lax.all_gather(local_velocity, 'rad', axis=2, tiled=True)  10.2 us
    transpose x1, local copies, waits for them, and re-layouts, on_device(): jnp.einsum('klt,rckl->trck', masked_table, levels, preferred_element_type...  9.72 us
  transfers between devices with their start and end apart: 8, of which 5 were waited for; matrix products, arithmetic and copies ran while one was open for 5% of the time, Pallas kernels for 0%

commit v1 on v0

v1 whole, which is shorter than its diff:
```python
import functools
import math

import jax
import jax.numpy as jnp
from jax import lax
from jax.experimental import pallas as pl
from jax.experimental.pallas import tpu as pltpu
from jax.sharding import PartitionSpec as P

L = 512
NPHI = 1024
QROWS = 16
MESH = pl.DeviceIdType.MESH


time_step = 0.05
composition_weight = 0.8


def synthesis_tables(order_table):
    longitude = jnp.arange(NPHI, dtype=jnp.int32)
    phase_index = order_table[:, None] * longitude[None, :] % NPHI
    angles = phase_index.astype(jnp.float32) * (2.0 * math.pi / NPHI)
    weights = jnp.where(order_table == 0, 1.0, 2.0).astype(jnp.float32) / math.sqrt(L)
    cosine = jnp.cos(angles) * weights[:, None]
    sine = jnp.sin(angles) * weights[:, None]
    slopes = (order_table.astype(jnp.float32) / L)[:, None]
    values = jnp.stack([cosine, -sine])
    turned = jnp.stack([-sine * slopes, -cosine * slopes])
    return jnp.concatenate([values, turned], axis=2).astype(jnp.bfloat16)


def column_kernel(rad_count, ma_count, partial_ref, sum_ref, velocity_ref, arrived, mine, beside, whole,
                  send_a, recv_a, send_b, recv_b, send_c, recv_c):
    r = lax.axis_index("rad")
    m = lax.axis_index("ma")
    total_rows, width = partial_ref.shape
    rows = total_rows // ma_count
    barrier = pltpu.get_barrier_semaphore()
    for d in range(1, ma_count):
        pl.semaphore_signal(
            barrier, inc=1, device_id={"ma": lax.rem(m + d, ma_count)}, device_id_type=MESH
        )
    for d in range(1, rad_count):
        pl.semaphore_signal(
            barrier, inc=1, device_id={"rad": lax.rem(r + d, rad_count)}, device_id_type=MESH
        )
    pl.semaphore_wait(barrier, ma_count + rad_count - 2)

    def block_of(index):
        return pl.ds(pl.multiple_of(index * rows, rows), rows)

    first = []
    for d in range(1, ma_count):
        peer = lax.rem(m + d, ma_count)
        copy = pltpu.make_async_remote_copy(
            src_ref=partial_ref.at[block_of(peer)],
            dst_ref=arrived.at[d - 1],
            send_sem=send_a.at[d - 1],
            recv_sem=recv_a.at[d - 1],
            device_id={"ma": peer},
            device_id_type=MESH,
        )
        copy.start()
        first.append(copy)
    mine[...] = partial_ref[block_of(m), :]
    for d in range(1, ma_count):
        first[d - 1].wait_recv()
        mine[...] += arrived[d - 1]
    second = []
    for d in range(1, rad_count):
        copy = pltpu.make_async_remote_copy(
            src_ref=mine,
            dst_ref=beside.at[d - 1],
            send_sem=send_b.at[d - 1],
            recv_sem=recv_b.at[d - 1],
            device_id={"rad": lax.rem(r + d, rad_count)},
            device_id_type=MESH,
        )
        copy.start()
        second.append(copy)
    total = mine[...]
    for d in range(1, rad_count):
        second[d - 1].wait_recv()
        total = total + beside[d - 1]
    whole[block_of(m), :] = total
    third = []
    for d in range(1, ma_count):
        copy = pltpu.make_async_remote_copy(
            src_ref=whole.at[block_of(m)],
            dst_ref=whole.at[block_of(m)],
            send_sem=send_c.at[d - 1],
            recv_sem=recv_c.at[d - 1],
            device_id={"ma": lax.rem(m + d, ma_count)},
            device_id_type=MESH,
        )
        copy.start()
        third.append(copy)
    sum_ref[...] = total
    for d in range(1, ma_count):
        sender = lax.rem(m + ma_count - d, ma_count)
        pltpu.make_async_remote_copy(
            src_ref=whole.at[block_of(sender)],
            dst_ref=whole.at[block_of(sender)],
            send_sem=send_c.at[d - 1],
            recv_sem=recv_c.at[d - 1],
            device_id={"ma": sender},
            device_id_type=MESH,
        ).wait_recv()
    for copy in first + second + third:
        copy.wait_send()
    value = whole[...]
    row = lax.broadcasted_iota(jnp.int32, (total_rows, 1), 0)
    radius = 0.35 + 0.65 * (row.astype(jnp.float32) + 0.5) / total_rows
    after = pltpu.roll(value, width - 1, 1)
    before = pltpu.roll(value, 1, 1)
    velocity_ref[0] = ((after - before) / (2.0 * radius)).astype(jnp.bfloat16)
    above = jnp.where(row == total_rows - 1, 0.0, pltpu.roll(value, total_rows - 1, 0))
    below = jnp.where(row == 0, 0.0, pltpu.roll(value, 1, 0))
    velocity_ref[1] = (-(above - below) * 0.5).astype(jnp.bfloat16)


def column_exchange(partial_value):
    rad_count = lax.axis_size("rad")
    ma_count = lax.axis_size("ma")
    total_rows, width = partial_value.shape
    rows = total_rows // ma_count
    dma = pltpu.SemaphoreType.DMA
    vmem = pl.BlockSpec(memory_space=pltpu.VMEM)
    summed, velocity = pl.pallas_call(
        functools.partial(column_kernel, rad_count, ma_count),
        out_shape=(
            jax.ShapeDtypeStruct((rows, width), jnp.float32),
            jax.ShapeDtypeStruct((2, total_rows, width), jnp.bfloat16),
        ),
        in_specs=[vmem],
        out_specs=(vmem, vmem),
        scratch_shapes=[
            pltpu.VMEM((ma_count - 1, rows, width), jnp.float32),
            pltpu.VMEM((rows, width), jnp.float32),
            pltpu.VMEM((rad_count - 1, rows, width), jnp.float32),
            pltpu.VMEM((total_rows, width), jnp.float32),
            dma((ma_count - 1,)),
            dma((ma_count - 1,)),
            dma((rad_count - 1,)),
            dma((rad_count - 1,)),
            dma((ma_count - 1,)),
            dma((ma_count - 1,)),
        ],
        compiler_params=pltpu.CompilerParams(collective_id=0, has_side_effects=True),
        name="column_exchange",
    )(partial_value)
    block = width // rad_count
    owned = lax.dynamic_slice_in_dim(summed, lax.axis_index("rad") * block, block, axis=1)
    return owned, velocity


def on_device(spectrum, radial_table, legendre, order_table, cylinder_row, column_weight):
    slot_count = spectrum.shape[1]
    degree_count = spectrum.shape[2]
    level_count = radial_table.shape[0]
    latitude_count = legendre.shape[2]
    rad_count = lax.axis_size("rad")
    ma_count = lax.axis_size("ma")
    total_rows = QROWS * ma_count
    my_orders = lax.dynamic_slice_in_dim(order_table, lax.axis_index("ma") * slot_count, slot_count)
    my_degrees = lax.axis_index("rad") * degree_count + jnp.arange(degree_count, dtype=jnp.int32)
    allowed = my_degrees[None, :] >= my_orders[:, None]
    masked_table = jnp.where(allowed[:, :, None], legendre, jnp.zeros_like(legendre))
    levels = jnp.einsum(
        "rn,ckln->rckl", radial_table, spectrum, preferred_element_type=jnp.float32
    ).astype(jnp.bfloat16)
    contribution = jnp.einsum(
        "klt,rckl->trck", masked_table, levels, preferred_element_type=jnp.float32
    )
    pieces = contribution.astype(jnp.bfloat16).reshape(
        rad_count, latitude_count // rad_count, level_count * 4 * slot_count
    )
    pieces = lax.all_to_all(pieces, "rad", split_axis=0, concat_axis=0, tiled=True)
    latitudes = jnp.sum(pieces.astype(jnp.float32), axis=0).astype(jnp.bfloat16)
    received = lax.all_to_all(latitudes, "ma", split_axis=0, concat_axis=1, tiled=True)
    lat_rows = received.shape[0]
    coefficients = received.reshape(lat_rows, ma_count, level_count, 2, 2, slot_count)
    tables = synthesis_tables(order_table).reshape(2, ma_count, slot_count, 2 * NPHI)
    synthesis = jnp.einsum(
        "tsrfik,iskq->ftrq", coefficients, tables, preferred_element_type=jnp.float32
    ).astype(jnp.bfloat16)
    fields = synthesis[..., :NPHI].astype(jnp.float32)
    slope_field = synthesis[..., NPHI:].astype(jnp.float32)
    buoyancy = fields[0] - composition_weight * fields[1]
    weighted = (column_weight[:, :, None] * buoyancy).reshape(-1, NPHI)
    point_rows = cylinder_row.reshape(-1)
    row_ids = jnp.arange(total_rows, dtype=jnp.int32)
    selector = (row_ids[:, None] == point_rows[None, :]).astype(jnp.float32)
    partial_value = jnp.dot(
        selector, weighted, precision=lax.Precision.HIGHEST, preferred_element_type=jnp.float32
    )
    owned, velocity = column_exchange(partial_value)
    chooser = (point_rows[:, None] == row_ids[None, :]).astype(jnp.bfloat16)
    moved = jnp.einsum("pj,cjq->cpq", chooser, velocity, preferred_element_type=jnp.float32)
    moved = moved.reshape(2, lat_rows, level_count, NPHI)
    inverse = 1.0 / (0.35 + 0.65 * (cylinder_row.astype(jnp.float32) + 0.5) / total_rows)
    advected = fields - time_step * inverse[None, :, :, None] * (
        moved[1][None] * slope_field + moved[0][None] * fields
    )
    return (owned, advected)


def solution(mesh):
    return jax.shard_map(
        on_device,
        mesh=mesh,
        in_specs=(
            P(None, "ma", "rad", None),
            P(),
            P("ma", "rad", None),
            P(),
            P(("rad", "ma"), None),
            P(("rad", "ma"), None),
        ),
        out_specs=(P("ma", "rad"), P(None, ("rad", "ma"), None, None)),
        check_vma=False,
    )
```

time: 281 us -> 165 us (0.59)
  waiting for transfers between devices: 170 us -> 0.01 us
  blocking collectives: 23.9 us -> 75.1 us
  Pallas kernels: 0 us -> 25.9 us
  between operations: 13.9 us -> 0.8 us
  starting transfers between devices: 13.8 us -> 5.48 us
    reduce_scatter x3 -> x0, waiting for transfers between devices: 167 us -> none  [the longest x1 113 us: on_device(): lax.psum_scatter(contribution.reshape(latitude_count // rad_count * lax.a...]
    all_to_all x0 -> x1, blocking collectives: none -> 75.1 us  [on_device(): lax.all_to_all(pieces, 'rad', split_axis=0, concat_axis=0, tiled=True)]
    pallas_call x0 -> x1, Pallas kernels: none -> 25.9 us  [column_exchange(): pl.pallas_call(functools.partial(column_kernel, rad_count, ma_count), out...]
    all_gather x2 -> x0, blocking collectives: 23.9 us -> none  [the longest x1 13.6 us: owner_velocity(): return lax.all_gather(velocity, 'ma', axis=1, tiled=True)]
    transpose x1 -> x0, local copies, waits for them, and re-layouts: 9.72 us -> none  [on_device(): jnp.einsum('klt,rckl->trck', masked_table, levels, preferred_element_type...]
    ppermute x4 -> x0, starting transfers between devices: 9.38 us -> none  [the longest x2 5.14 us: padded(): lax.ppermute(lax.slice_in_dim(block, 0, width, axis=dim), axis, backward)]
    reshape x0 -> x2, local copies, waits for them, and re-layouts: none -> 5.31 us  [on_device(): contribution.astype(jnp.bfloat16)]
    ppermute x4 -> x0, waiting for transfers between devices: 3.05 us -> none  [the longest x2 1.84 us: padded(): lax.ppermute(lax.slice_in_dim(block, block.shape[dim] - width, None, axis...]
  transfers between devices with their start and end apart: 8 -> 1, of which waited for: 5 -> 0; matrix products, arithmetic and copies ran while one was open for 5% -> 7% of each run, Pallas kernels for 0% -> 0%
where the time goes in v1:
time: 165 us
  blocking collectives  75.1 us (46%)
  Pallas kernels  25.9 us (16%)
  matrix products  23.4 us (14%)
  local copies, waits for them, and re-layouts  20.3 us (12%)
  other arithmetic  14 us (8%)
  starting transfers between devices  5.48 us (3%)
    all_to_all x1, blocking collectives, on_device(): lax.all_to_all(pieces, 'rad', split_axis=0, concat_axis=0, tiled=True)  75.1 us
    pallas_call x1, Pallas kernels, column_exchange(): pl.pallas_call(functools.partial(column_kernel, rad_count, ma_count), out...  25.9 us
    dot_general x1, matrix products, on_device(): jnp.einsum('klt,rckl->trck', masked_table, levels, preferred_element_type...  16.1 us
    another operation x1, other arithmetic  11.5 us
    all_to_all x1, starting transfers between devices, on_device(): lax.all_to_all(latitudes, 'ma', split_axis=0, concat_axis=1, tiled=True)  5.48 us
    reshape x2, local copies, waits for them, and re-layouts, on_device(): contribution.astype(jnp.bfloat16)  5.31 us
    dot_general x1, matrix products, on_device(): jnp.einsum('tsrfik,iskq->ftrq', coefficients, tables, preferred_element_t...  4.47 us
    convert_element_type x1, local copies, waits for them, and re-layouts, on_device(): contribution.astype(jnp.bfloat16)  3.94 us
  transfers between devices with their start and end apart: 1, of which 0 were waited for; matrix products, arithmetic and copies ran while one was open for 7% of the time, Pallas kernels for 0%

profile of v1, /device:TPU:1, one launch (start us, length us, event | category | flops | bytes accessed | tf_op | source)
XLA Modules:
  0.0 164.9 jit_solution(6106669826786677809)
XLA Ops:
  0.6 0.0 copy-start
  0.7 0.8 dynamic_slice.6
  1.4 0.1 broadcast_compare_fusion
  1.5 0.0 copy-done
  1.5 16.1 %convert_bitcast_fusion = bf16[512,12,4,64]{0,1,2,3:T(8,128)(2,1)} fusion(bf16[64,128,512]{2,1,0:T(8,128)(2,1)} %param.8, pred[64,128]{1,0:T(8,128)(4,1)S(1)} %broadcast_compare_fusion, bf16[4,64,128,384]{3,2,1,0:T(8,128)(2,1)} %param.6, bf16[12,384]{1,0:T(8,128)(2,1)S(1)} %copy-done), kind=kOutput, calls=%fused_computation.14 | convolution fusion | flops 710803456 | bytes 36717568 | tf_op jit(solution)/shard_map/klt,rckl->trck/dot_general | solution.py:174
  17.6 3.9 %copy.29 = bf16[512,12,4,64]{0,3,2,1:T(8,128)(2,1)S(1)} copy(bf16[512,12,4,64]{0,1,2,3:T(8,128)(2,1)} %convert_bitcast_fusion) | data formatting | bytes 6291456 | tf_op jit(solution)/shard_map/convert_element_type | solution.py:177
  21.5 3.0 %reshape.276 = bf16[4,128,3072]{1,0,2:T(4,128)(2,1)} reshape(bf16[512,12,4,64]{0,3,2,1:T(8,128)(2,1)S(1)} %copy.29) | data formatting | bytes 6291456 | tf_op jit(solution)/shard_map/reshape | solution.py:177
  24.6 2.3 %copy.30 = bf16[4,128,3072]{1,2,0:T(8,128)(2,1)S(1)} copy(bf16[4,128,3072]{1,0,2:T(4,128)(2,1)} %reshape.276) | data formatting | bytes 6291456 | tf_op jit(solution)/shard_map/reshape | solution.py:177
  26.8 75.1 %all_to_all.21 = bf16[4,128,3072]{1,2,0:T(8,128)(2,1)S(1)} all-to-all(bf16[4,128,3072]{1,2,0:T(8,128)(2,1)S(1)} %copy.30), channel_id=1, replica_groups=mesh['rad'=4,'ma'=8] {'rad'}, dimensions={0} | all-to-all | bytes 6291456 | tf_op jit(solution)/shard_map/all_to_all | solution.py:180
  101.9 1.5 reduce_sum.12
  103.5 0.0 copy-start.3
  103.5 0.0 copy-start.2
  103.5 0.0 copy-start.4
  103.5 2.3 %copy.32 = bf16[128,3072]{1,0:T(8,128)(2,1)} copy(bf16[128,3072]{0,1:T(8,128)(2,1)} %reduce_sum.12) | data formatting | bytes 1572864 | tf_op jit(solution)/shard_map/reduce_sum | solution.py:181
  105.8 5.5 %all-to-all-start.1 = ((bf16[8,16,3072]{2,1,0:T(8,128)(2,1)}), bf16[8,16,3072]{2,1,0:T(8,128)(2,1)S(1)}, u32[]{:S(2)}, u32[]{:S(2)}) async-start(bf16[8,16,3072]{2,1,0:T(8,128)(2,1)} %bitcast.6), calls=%async_computation.1 | async-start | bytes 1572864 | tf_op jit(solution)/shard_map/all_to_all | solution.py:182
  111.3 0.0 copy-done.3
  111.3 0.1 mul.208
  111.4 0.1 mul.214
  111.5 0.1 mul.218
  111.5 0.0 copy-done.2
  111.5 0.1 eq.37
  111.6 0.0 copy-done.4
  111.6 0.1 mul.206
  111.7 0.1 copy.36
  111.8 11.5 %fusion.23 = (bf16[1,8,64,1024]{3,2,1,0:T(8,128)(2,1)}, bf16[1,8,64,1024]{3,2,1,0:T(8,128)(2,1)}, bf16[1,8,64,1024]{3,2,1,0:T(8,128)(2,1)}, bf16[1,8,64,1024]{3,2,1,0:T(8,128)(2,1)}) fusion(f32[8,64]{1,0:T(8,128)S(1)} %mul.214, s32[8,64]{1,0:T(8,128)S(1)} %mul.208, f32[8,64]{1,0:T(8,128)S(1)} %mul.218), kind=kLoop, calls=%fused_computation.31 | loop fusion | flops 12582912 | bytes 4200448 | tf_op jit(solution)/shard_map/convert.5
  123.3 0.0 all-to-all-done.1
  123.3 1.0 reshape.283
  124.4 4.5 %fusion.16 = bf16[2,16,12,2048]{3,1,0,2:T(8,128)(2,1)S(1)} fusion(bf16[1,8,64,1024]{3,2,1,0:T(8,128)(2,1)} %get-tuple-element.20, bf16[1,8,64,1024]{3,2,1,0:T(8,128)(2,1)} %get-tuple-element.21, bf16[1,8,64,1024]{3,2,1,0:T(8,128)(2,1)} %get-tuple-element.19, bf16[1,8,64,1024]{3,2,1,0:T(8,128)(2,1)} %get-tuple-element.18, ...), kind=kOutput, calls=%fused_computation.20 | convolution fusion | flops 1628176384 | bytes 6553600 | tf_op jit(solution)/shard_map/tsrfik,iskq->ftrq/dot_general | solution.py:186
  128.8 0.2 slice_convert_fusion
  129.0 0.1 fusion.29
  129.2 0.5 copy.35
  129.6 0.1 sub.11
  129.7 1.4 fusion.30.partial_ref
  131.1 25.9 %column_exchange.1 = (f32[16,1024]{1,0:T(8,128)}, bf16[2,128,1024]{2,1,0:T(8,128)(2,1)}) custom-call(f32[128,1024]{1,0:T(8,128)} %fusion.30.partial_ref), custom_call_target="tpu_custom_call" | custom-call | tf_op jit(solution)/shard_map/column_exchange/pallas_call | solution.py:131
  157.0 1.4 convolution_bitcast_fusion
  158.5 1.0 fusion.43
  159.5 0.1 mul.231
  159.6 0.5 copy.37
  160.1 1.2 mul.234
  161.3 0.5 copy.38
  161.8 0.0 copy-start.1
  161.8 0.5 multiply_subtract_fusion
  162.3 1.2 copy.39
  163.6 1.3 constant_dynamic-slice_fusion
  164.9 0.0 copy-done.1
  (3 shorter events, 0.0 us)
Async XLA Ops:
  0.6 0.9 copy-start
  103.5 7.8 %copy-start.3 = (s32[512]{0:T(512)S(1)}, s32[512]{0:T(512)}, u32[]{:S(2)}) copy-start(s32[512]{0:T(512)} %param.9) | copy-start | bytes 6148
  103.5 8.1 %copy-start.2 = (s32[16,12]{1,0:T(8,128)S(1)}, s32[16,12]{1,0:T(8,128)}, u32[]{:S(2)}) copy-start(s32[16,12]{1,0:T(8,128)} %param.10) | copy-start | bytes 2308
  103.5 8.1 %copy-start.4 = (f32[16,12]{1,0:T(8,128)S(1)}, f32[16,12]{1,0:T(8,128)}, u32[]{:S(2)}) copy-start(f32[16,12]{1,0:T(8,128)} %param.11) | copy-start | bytes 2308
  105.8 17.5 %all-to-all-start.1 = ((bf16[8,16,3072]{2,1,0:T(8,128)(2,1)}), bf16[8,16,3072]{2,1,0:T(8,128)(2,1)S(1)}, u32[]{:S(2)}, u32[]{:S(2)}) async-start(bf16[8,16,3072]{2,1,0:T(8,128)(2,1)} %bitcast.6), calls=%async_computation.1 | async-start | bytes 1572864 | tf_op jit(solution)/shard_map/all_to_all | solution.py:182
  161.8 3.1 %copy-start.1 = (bf16[12,384]{1,0:T(8,128)(2,1)S(1)}, bf16[12,384]{1,0:T(8,128)(2,1)}, u32[]{:S(2)}) copy-start(bf16[12,384]{1,0:T(8,128)(2,1)} %param.7) | copy-start | bytes 27652

commit v2 on v1

--- a/solution.py
+++ b/solution.py
@@ -11,6 +11,8 @@
 L = 512
 NPHI = 1024
 QROWS = 16
+LANES = 128
+GROUP = 8
 MESH = pl.DeviceIdType.MESH
 
 
@@ -19,16 +21,259 @@
 
 
 def synthesis_tables(order_table):
-    longitude = jnp.arange(NPHI, dtype=jnp.int32)
-    phase_index = order_table[:, None] * longitude[None, :] % NPHI
-    angles = phase_index.astype(jnp.float32) * (2.0 * math.pi / NPHI)
+    def turn(steps):
+        phase_index = order_table[:, None] * steps[None, :] % NPHI
+        angles = phase_index.astype(jnp.float32) * (2.0 * math.pi / NPHI)
+        return jnp.cos(angles), jnp.sin(angles)
+
+    near_cos, near_sin = turn(jnp.arange(LANES, dtype=jnp.int32))
+    far_cos, far_sin = turn(jnp.arange(NPHI // LANES, dtype=jnp.int32) * LANES)
     weights = jnp.where(order_table == 0, 1.0, 2.0).astype(jnp.float32) / math.sqrt(L)
-    cosine = jnp.cos(angles) * weights[:, None]
-    sine = jnp.sin(angles) * weights[:, None]
-    slopes = (order_table.astype(jnp.float32) / L)[:, None]
+    far_cos = (far_cos * weights[:, None])[:, :, None]
+    far_sin = (far_sin * weights[:, None])[:, :, None]
+    near_cos = near_cos[:, None, :]
+    near_sin = near_sin[:, None, :]
+    cosine = far_cos * near_cos - far_sin * near_sin
+    sine = far_sin * near_cos + far_cos * near_sin
+    slopes = (order_table.astype(jnp.float32) / L)[:, None, None]
     values = jnp.stack([cosine, -sine])
     turned = jnp.stack([-sine * slopes, -cosine * slopes])
-    return jnp.concatenate([values, turned], axis=2).astype(jnp.bfloat16)
+    tables = jnp.concatenate([values, turned], axis=2).astype(jnp.bfloat16)
+    return tables.reshape(2, order_table.shape[0], 2 * NPHI)
+
+
+def latitude_kernel(rad_count, ma_count, chunks, mask_ref, radial_ref, spectrum_ref, legendre_ref, out_ref,
+                    spectrum_buf, legendre_buf, own, out_up, out_down, in_up, in_down, ready, arrived,
+                    fetch_sem, up_send, up_recv, down_send, down_recv, ma_send, ma_recv):
+    r = lax.axis_index("rad")
+    m = lax.axis_index("ma")
+    last = rad_count - 1
+    _, _, slots, degrees, modes = spectrum_buf.shape
+    rows = radial_ref.shape[1]
+    lanes = own.shape[3]
+    share = out_ref.shape[2]
+
+    def fetch(c, slot):
+        piece = pl.ds(c * slots, slots)
+        return (
+            pltpu.make_async_copy(
+                spectrum_ref.at[:, piece], spectrum_buf.at[slot], fetch_sem.at[0, slot]
+            ),
+            pltpu.make_async_copy(
+                legendre_ref.at[piece], legendre_buf.at[slot], fetch_sem.at[1, slot]
+            ),
+        )
+
+    for copy in fetch(0, 0):
+        copy.start()
+
+    barrier = pltpu.get_barrier_semaphore()
+    for d in range(1, ma_count):
+        pl.semaphore_signal(
+            barrier, inc=1, device_id={"ma": lax.rem(m + d, ma_count)}, device_id_type=MESH
+        )
+    for d in range(1, rad_count):
+        pl.semaphore_signal(
+            barrier, inc=1, device_id={"rad": lax.rem(r + d, rad_count)}, device_id_type=MESH
+        )
+    pl.semaphore_wait(barrier, ma_count + rad_count - 2)
+
+    def up(c, target):
+        return pltpu.make_async_remote_copy(
+            src_ref=out_up.at[c, target],
+            dst_ref=in_up.at[c, target],
+            send_sem=up_send.at[c, target],
+            recv_sem=up_recv.at[c, target],
+            device_id={"rad": lax.rem(r + 1, rad_count)},
+            device_id_type=MESH,
+        )
+
+    def down(c, target):
+        return pltpu.make_async_remote_copy(
+            src_ref=out_down.at[c, target],
+            dst_ref=in_down.at[c, target],
+            send_sem=down_send.at[c, target],
+            recv_sem=down_recv.at[c, target],
+            device_id={"rad": lax.rem(r + last, rad_count)},
+            device_id_type=MESH,
+        )
+
+    def hand_over(c, d):
+        peer = lax.rem(m + d, ma_count)
+        return pltpu.make_async_remote_copy(
+            src_ref=ready.at[c, pl.ds(pl.multiple_of(peer * share, share), share)],
+            dst_ref=arrived.at[m, c],
+            send_sem=ma_send.at[c, d - 1],
+            recv_sem=ma_recv.at[c, d - 1],
+            device_id={"ma": peer},
+            device_id_type=MESH,
+        )
+
+    def compute(c, carry):
+        slot = lax.rem(c, 2)
+
+        @pl.when(c + 1 < chunks)
+        def _():
+            for copy in fetch(c + 1, 1 - slot):
+                copy.start()
+
+        for copy in fetch(c, slot):
+            copy.wait()
+        levels = jnp.zeros((rows, slots * degrees), jnp.float32)
+        for part in range(spectrum_buf.shape[1]):
+            levels += lax.dot_general(
+                radial_ref[part],
+                spectrum_buf[slot, part].reshape(slots * degrees, modes),
+                (((1,), (1,)), ((), ())),
+                preferred_element_type=jnp.float32,
+            )
+        for s in range(slots):
+            kept = levels[:, s * degrees : (s + 1) * degrees] * mask_ref[c * slots + s]
+            sums = jnp.dot(
+                kept.astype(jnp.bfloat16), legendre_buf[slot, s], preferred_element_type=jnp.float32
+            )
+            for target in range(rad_count):
+                own[c, target, s * rows : (s + 1) * rows, :] = sums[
+                    :, target * lanes : (target + 1) * lanes
+                ]
+
+        @pl.when(r == 0)
+        def _():
+            for target in range(last, 0, -1):
+                out_up[c, target] = own[c, target].astype(jnp.bfloat16)
+                up(c, target).start()
+
+        @pl.when(r == last)
+        def _():
+            for target in range(last):
+                out_down[c, target] = own[c, target].astype(jnp.bfloat16)
+                down(c, target).start()
+
+        return carry
+
+    lax.fori_loop(0, chunks, compute, 0)
+
+    def relay(c):
+        for target in range(last, 0, -1):
+
+            @pl.when((r > 0) & (r < target))
+            def _():
+                up(c, target).wait_recv()
+                out_up[c, target] = (
+                    own[c, target] + in_up[c, target].astype(jnp.float32)
+                ).astype(jnp.bfloat16)
+                up(c, target).start()
+
+        for target in range(last):
+
+            @pl.when((r < last) & (r > target))
+            def _():
+                down(c, target).wait_recv()
+                out_down[c, target] = (
+                    own[c, target] + in_down[c, target].astype(jnp.float32)
+                ).astype(jnp.bfloat16)
+                down(c, target).start()
+
+    def finish(c):
+        @pl.when(r > 0)
+        def _():
+            up(c, r).wait_recv()
+            own[c, r] += in_up[c, r].astype(jnp.float32)
+
+        @pl.when(r < last)
+        def _():
+            down(c, r).wait_recv()
+            own[c, r] += in_down[c, r].astype(jnp.float32)
+
+        ready[c] = own[c, r].T.astype(jnp.bfloat16)
+        for d in range(1, ma_count):
+            hand_over(c, d).start()
+        arrived[m, c] = ready[c, pl.ds(pl.multiple_of(m * share, share), share), :]
+
+    def pass_on(c, carry):
+        relay(c)
+
+        @pl.when(c > 0)
+        def _():
+            finish(c - 1)
+
+        return carry
+
+    lax.fori_loop(0, chunks, pass_on, 0)
+    finish(chunks - 1)
+
+    def drain(c, carry):
+        for d in range(1, ma_count):
+            sender = lax.rem(m + ma_count - d, ma_count)
+            pltpu.make_async_remote_copy(
+                src_ref=ready.at[c, pl.ds(0, share)],
+                dst_ref=arrived.at[sender, c],
+                send_sem=ma_send.at[c, d - 1],
+                recv_sem=ma_recv.at[c, d - 1],
+                device_id={"ma": sender},
+                device_id_type=MESH,
+            ).wait_recv()
+            hand_over(c, d).wait_send()
+        for target in range(rad_count):
+
+            @pl.when(r < target)
+            def _():
+                up(c, target).wait_send()
+
+            @pl.when(r > target)
+            def _():
+                down(c, target).wait_send()
+
+        return carry
+
+    lax.fori_loop(0, chunks, drain, 0)
+    out_ref[...] = arrived[...]
+
+
+def latitude_exchange(spectrum, radial_table, legendre, allowed, slots):
+    rad_count = lax.axis_size("rad")
+    ma_count = lax.axis_size("ma")
+    parts, slot_count, degrees, modes = spectrum.shape
+    level_count = radial_table.shape[0]
+    latitude_count = legendre.shape[2]
+    rows = level_count * parts
+    chunks = slot_count // slots
+    lanes = latitude_count // rad_count
+    share = lanes // ma_count
+    spread = jnp.einsum("rn,cd->crdn", radial_table, jnp.eye(parts, dtype=radial_table.dtype))
+    spread = spread.reshape(parts, rows, modes)
+    dma = pltpu.SemaphoreType.DMA
+    vmem = pl.BlockSpec(memory_space=pltpu.VMEM)
+    hbm = pl.BlockSpec(memory_space=pl.ANY)
+    travelling = pltpu.VMEM((chunks, rad_count, slots * rows, lanes), jnp.bfloat16)
+    return pl.pallas_call(
+        functools.partial(latitude_kernel, rad_count, ma_count, chunks),
+        out_shape=jax.ShapeDtypeStruct((ma_count, chunks, share, slots * rows), jnp.bfloat16),
+        in_specs=[vmem, vmem, hbm, hbm],
+        out_specs=vmem,
+        scratch_shapes=[
+            pltpu.VMEM((2, parts, slots, degrees, modes), jnp.bfloat16),
+            pltpu.VMEM((2, slots, degrees, latitude_count), jnp.bfloat16),
+            pltpu.VMEM((chunks, rad_count, slots * rows, lanes), jnp.float32),
+            travelling,
+            travelling,
+            travelling,
+            travelling,
+            pltpu.VMEM((chunks, lanes, slots * rows), jnp.bfloat16),
+            pltpu.VMEM((ma_count, chunks, share, slots * rows), jnp.bfloat16),
+            dma((2, 2)),
+            dma((chunks, rad_count)),
+            dma((chunks, rad_count)),
+            dma((chunks, rad_count)),
+            dma((chunks, rad_count)),
+            dma((chunks, ma_count - 1)),
+            dma((chunks, ma_count - 1)),
+        ],
+        compiler_params=pltpu.CompilerParams(
+            collective_id=1, has_side_effects=True, vmem_limit_bytes=56 * 1024 * 1024
+        ),
+        name="latitude_exchange",
+    )(allowed.astype(jnp.float32)[:, None, :], spread, spectrum, legendre)
 
 
 def column_kernel(rad_count, ma_count, partial_ref, sum_ref, velocity_ref, arrived, mine, beside, whole,
@@ -167,24 +412,40 @@
     my_orders = lax.dynamic_slice_in_dim(order_table, lax.axis_index("ma") * slot_count, slot_count)
     my_degrees = lax.axis_index("rad") * degree_count + jnp.arange(degree_count, dtype=jnp.int32)
     allowed = my_degrees[None, :] >= my_orders[:, None]
-    masked_table = jnp.where(allowed[:, :, None], legendre, jnp.zeros_like(legendre))
-    levels = jnp.einsum(
-        "rn,ckln->rckl", radial_table, spectrum, preferred_element_type=jnp.float32
-    ).astype(jnp.bfloat16)
-    contribution = jnp.einsum(
-        "klt,rckl->trck", masked_table, levels, preferred_element_type=jnp.float32
-    )
-    pieces = contribution.astype(jnp.bfloat16).reshape(
-        rad_count, latitude_count // rad_count, level_count * 4 * slot_count
-    )
-    pieces = lax.all_to_all(pieces, "rad", split_axis=0, concat_axis=0, tiled=True)
-    latitudes = jnp.sum(pieces.astype(jnp.float32), axis=0).astype(jnp.bfloat16)
-    received = lax.all_to_all(latitudes, "ma", split_axis=0, concat_axis=1, tiled=True)
-    lat_rows = received.shape[0]
-    coefficients = received.reshape(lat_rows, ma_count, level_count, 2, 2, slot_count)
-    tables = synthesis_tables(order_table).reshape(2, ma_count, slot_count, 2 * NPHI)
+    tables = synthesis_tables(order_table)
+    lat_rows = latitude_count // (rad_count * ma_count)
+    if (
+        latitude_count % (rad_count * LANES) == 0
+        and degree_count % LANES == 0
+        and slot_count % GROUP == 0
+        and GROUP * level_count * 4 % LANES == 0
+        and lat_rows % 16 == 0
+    ):
+        received = latitude_exchange(spectrum, radial_table, legendre, allowed, GROUP)
+        coefficients = received.reshape(
+            ma_count, slot_count // GROUP, lat_rows, GROUP, level_count, 2, 2
+        )
+        coefficients = coefficients.transpose(2, 4, 5, 6, 0, 1, 3)
+        coefficients = coefficients.reshape(lat_rows, level_count, 2, 2, ma_count * slot_count)
+    else:
+        masked_table = jnp.where(allowed[:, :, None], legendre, jnp.zeros_like(legendre))
+        levels = jnp.einsum(
+            "rn,ckln->rckl", radial_table, spectrum, preferred_element_type=jnp.float32
+        ).astype(jnp.bfloat16)
+        contribution = jnp.einsum(
+            "klt,rckl->trck", masked_table, levels, preferred_element_type=jnp.float32
+        )
+        pieces = contribution.astype(jnp.bfloat16).reshape(
+            rad_count, latitude_count // rad_count, level_count * 4 * slot_count
+        )
+        pieces = lax.all_to_all(pieces, "rad", split_axis=0, concat_axis=0, tiled=True)
+        latitudes = jnp.sum(pieces.astype(jnp.float32), axis=0).astype(jnp.bfloat16)
+        received = lax.all_to_all(latitudes, "ma", split_axis=0, concat_axis=1, tiled=True)
+        coefficients = received.reshape(lat_rows, ma_count, level_count, 2, 2, slot_count)
+        coefficients = coefficients.transpose(0, 2, 3, 4, 1, 5)
+        coefficients = coefficients.reshape(lat_rows, level_count, 2, 2, ma_count * slot_count)
     synthesis = jnp.einsum(
-        "tsrfik,iskq->ftrq", coefficients, tables, preferred_element_type=jnp.float32
+        "trfik,ikq->ftrq", coefficients, tables, preferred_element_type=jnp.float32
     ).astype(jnp.bfloat16)
     fields = synthesis[..., :NPHI].astype(jnp.float32)
     slope_field = synthesis[..., NPHI:].astype(jnp.float32)

time: 165 us -> 171 us (1.036)
  Pallas kernels: 25.9 us -> 116 us
  blocking collectives: 75.1 us -> 0 us
  local copies, waits for them, and re-layouts: 20.3 us -> 35.8 us
  matrix products: 23.4 us -> 9.06 us
  starting transfers between devices: 5.48 us -> 0 us
  other arithmetic: 14 us -> 9.2 us
    pallas_call x0 -> x1, Pallas kernels: none -> 90.5 us  [latitude_exchange(): pl.pallas_call(functools.partial(latitude_kernel, rad_count, ma_count, ch...]
    all_to_all x1 -> x0, blocking collectives: 75.1 us -> none  [on_device(): lax.all_to_all(pieces, 'rad', split_axis=0, concat_axis=0, tiled=True)]
    dot_general x2 -> x1, matrix products: 20.5 us -> 6.25 us  [on_device(): jnp.einsum('trfik,ikq->ftrq', coefficients, tables, preferred_element_typ...]
    transpose x0 -> x1, local copies, waits for them, and re-layouts: none -> 12.7 us  [on_device(): coefficients = coefficients.transpose(2, 4, 5, 6, 0, 1, 3)]
    another operation x1 -> x2, other arithmetic: 11.5 us -> 1.99 us
    pallas_call x0 -> x1, local copies, waits for them, and re-layouts: none -> 6.38 us  [latitude_exchange(): pl.pallas_call(functools.partial(latitude_kernel, rad_count, ma_count, ch...]
    reshape x3 -> x1, local copies, waits for them, and re-layouts: 6.34 us -> 0.7 us  [latitude_exchange(): spread = spread.reshape(parts, rows, modes)]
    all_to_all x1 -> x0, starting transfers between devices: 5.48 us -> none  [on_device(): lax.all_to_all(latitudes, 'ma', split_axis=0, concat_axis=1, tiled=True)]
  transfers between devices with their start and end apart: 1 -> 0, of which waited for: 0 -> 0; matrix products, arithmetic and copies ran while one was open for 7% -> 0% of each run, Pallas kernels for 0% -> 0%
where the time goes in v2:
time: 171 us; the launch traced here: 170 us
  Pallas kernels  116 us (68%)
  local copies, waits for them, and re-layouts  35.8 us (21%)
  other arithmetic  9.2 us (5%)
  matrix products  9.06 us (5%)
    pallas_call x1, Pallas kernels, latitude_exchange(): pl.pallas_call(functools.partial(latitude_kernel, rad_count, ma_count, ch...  90.5 us
    pallas_call x1, Pallas kernels, column_exchange(): pl.pallas_call(functools.partial(column_kernel, rad_count, ma_count), out...  25.1 us
    transpose x1, local copies, waits for them, and re-layouts, on_device(): coefficients = coefficients.transpose(2, 4, 5, 6, 0, 1, 3)  12.7 us
    convert_element_type x1, local copies, waits for them, and re-layouts, synthesis_tables(): tables = jnp.concatenate([values, turned], axis=2).astype(jnp.bfloat16)  7.31 us
    pallas_call x1, local copies, waits for them, and re-layouts, latitude_exchange(): pl.pallas_call(functools.partial(latitude_kernel, rad_count, ma_count, ch...  6.38 us
    dot_general x1, matrix products, on_device(): jnp.einsum('trfik,ikq->ftrq', coefficients, tables, preferred_element_typ...  6.25 us

profile of v2, /device:TPU:1, one launch (start us, length us, event | category | flops | bytes accessed | tf_op | source)
XLA Modules:
  0.0 170.5 jit_solution(295670915596937015)
XLA Ops:
  0.7 0.8 dynamic_slice.6
  1.4 0.8 compare_convert_fusion.mask_ref
  2.2 0.8 multiply_bitcast_fusion
  3.0 0.7 reshape.262.radial_ref
  3.7 90.5 %latitude_exchange.1 = bf16[8,8,16,384]{3,2,1,0:T(8,128)(2,1)} custom-call(f32[64,1,128]{2,1,0:T(1,128)} %compare_convert_fusion.mask_ref, bf16[4,48,384]{2,1,0:T(8,128)(2,1)} %reshape.262.radial_ref, bf16[4,64,128,384]{3,2,1,0:T(8,128)(2,1)} %spectrum_ref.1, bf16[64,128,512]{2,1,0:T(8,128)(2,1)} %legendre_ref.1), custom_call_target="tpu_custom_call" | custom-call | tf_op jit(solution)/shard_map/latitude_exchange/pallas_call | solution.py:249
  94.2 6.4 %copy.24 = bf16[8,8,16,384]{2,1,3,0:T(8,128)(2,1)} copy(bf16[8,8,16,384]{3,2,1,0:T(8,128)(2,1)} %latitude_exchange.1) | data formatting | bytes 1572864 | tf_op jit(solution)/shard_map/latitude_exchange/pallas_call | solution.py:249
  100.6 0.0 copy-start.1
  100.6 12.7 %copy.25 = bf16[16,12,2,2,8,8,8]{0,6,5,4,3,2,1:T(8,128)(2,1)} copy(bf16[16,12,2,2,8,8,8]{0,5,3,2,1,6,4:T(8,128)(2,1)} %bitcast.30) | data formatting | bytes 1572864 | tf_op jit(solution)/shard_map/transpose | solution.py:428
  113.3 0.0 copy-done.1
  113.3 1.1 fusion.20
  114.5 0.2 cosine_multiply_fusion
  114.6 0.1 copy.22
  114.8 0.1 copy.21
  114.9 2.0 %fusion.8 = (bf16[1,512,8,128]{3,2,1,0:T(8,128)(2,1)S(1)}, bf16[1,512,8,128]{3,2,1,0:T(8,128)(2,1)S(1)}, bf16[1,512,8,128]{3,2,1,0:T(8,128)(2,1)S(1)}, bf16[1,512,8,128]{3,2,1,0:T(8,128)(2,1)S(1)}) fusion(f32[512,128]{1,0:T(8,128)S(1)} %get-tuple-element.23, f32[512,8]{1,0:T(8,128)S(1)} %copy.22, f32[512,128]{1,0:T(8,128)S(1)} %get-tuple-element.22, ...), kind=kLoop, calls=%fused_computation.10 | loop fusion | flops 7340032 | bytes 4753408 | tf_op jit(solution)/shard_map/convert.5
  116.9 2.4 %maximum_maximum_fusion = bf16[2,512,16,128]{3,2,1,0:T(8,128)(2,1)} fusion(bf16[1,512,8,128]{3,2,1,0:T(8,128)(2,1)S(1)} %get-tuple-element.18, bf16[1,512,8,128]{3,2,1,0:T(8,128)(2,1)S(1)} %get-tuple-element.19, bf16[1,512,8,128]{3,2,1,0:T(8,128)(2,1)S(1)} %get-tuple-element.17, bf16[1,512,8,128]{3,2,1,0:T(8,128)(2,1)S(1)} %get-tuple-element.16), kind=kLoop, calls=%fused_computation | loop fusion | flops 16777216 | bytes 8388608 | tf_op jit(solution)/shard_map/concatenate | solution.py:41
  119.3 7.3 %reshape.265 = bf16[2,512,2048,1,1]{2,1,0,3,4:T(8,128)(2,1)} reshape(bf16[2,512,16,128]{3,2,1,0:T(8,128)(2,1)} %maximum_maximum_fusion) | data formatting | bytes 8388608 | tf_op jit(solution)/shard_map/convert_element_type | solution.py:41
  126.6 6.3 %fusion.4 = bf16[2,16,12,2048]{3,1,0,2:T(8,128)(2,1)S(1)} fusion(bf16[16,12,2,2,512]{0,4,3,2,1:T(8,128)(2,1)} %bitcast.31, bf16[2,512,2048,1,1]{2,1,0,3,4:T(8,128)(2,1)} %reshape.265), kind=kOutput, calls=%fused_computation.4 | convolution fusion | flops 1611399168 | bytes 6553600 | tf_op jit(solution)/shard_map/trfik,ikq->ftrq/dot_general | solution.py:447
  132.9 0.2 slice_convert_fusion
  133.1 0.1 fusion.9
  133.2 0.0 copy-start.2
  133.2 0.0 copy-start
  133.2 0.5 copy.27
  133.7 0.1 sub.26
  133.8 0.1 copy-done.2
  133.9 0.1 mul.276
  134.0 0.0 copy-done
  134.0 0.1 eq.42
  134.1 1.4 fusion.10.partial_ref
  135.5 25.1 %column_exchange.1 = (f32[16,1024]{1,0:T(8,128)}, bf16[2,128,1024]{2,1,0:T(8,128)(2,1)}) custom-call(f32[128,1024]{1,0:T(8,128)} %fusion.10.partial_ref), custom_call_target="tpu_custom_call" | custom-call | tf_op jit(solution)/shard_map/column_exchange/pallas_call | solution.py:376
  160.6 1.3 constant_dynamic-slice_fusion
  161.9 1.4 convolution_bitcast_fusion
  163.4 1.0 fusion.29
  164.4 0.1 mul.315
  164.5 0.5 copy.30
  164.9 1.2 mul.312
  166.2 1.3 copy.29
  167.5 0.1 copy.28
  167.6 1.6 multiply_subtract_fusion.1
  169.2 1.2 copy.31
  (6 shorter events, 0.0 us)
Async XLA Ops:
  100.6 12.8 %copy-start.1 = (s32[512]{0:T(512)S(1)}, s32[512]{0:T(512)}, u32[]{:S(2)}) copy-start(s32[512]{0:T(512)} %param.9) | copy-start | bytes 6148
  133.2 0.7 copy-start.2
  133.2 0.8 copy-start

commit v3 on v2

--- a/solution.py
+++ b/solution.py
@@ -13,6 +13,7 @@
 QROWS = 16
 LANES = 128
 GROUP = 8
+HALVES = 2
 MESH = pl.DeviceIdType.MESH
 
 
@@ -29,21 +30,43 @@
     near_cos, near_sin = turn(jnp.arange(LANES, dtype=jnp.int32))
     far_cos, far_sin = turn(jnp.arange(NPHI // LANES, dtype=jnp.int32) * LANES)
     weights = jnp.where(order_table == 0, 1.0, 2.0).astype(jnp.float32) / math.sqrt(L)
-    far_cos = (far_cos * weights[:, None])[:, :, None]
-    far_sin = (far_sin * weights[:, None])[:, :, None]
-    near_cos = near_cos[:, None, :]
-    near_sin = near_sin[:, None, :]
-    cosine = far_cos * near_cos - far_sin * near_sin
-    sine = far_sin * near_cos + far_cos * near_sin
-    slopes = (order_table.astype(jnp.float32) / L)[:, None, None]
-    values = jnp.stack([cosine, -sine])
-    turned = jnp.stack([-sine * slopes, -cosine * slopes])
-    tables = jnp.concatenate([values, turned], axis=2).astype(jnp.bfloat16)
-    return tables.reshape(2, order_table.shape[0], 2 * NPHI)
+    far_cos = far_cos * weights[:, None]
+    far_sin = far_sin * weights[:, None]
+    slopes = (order_table.astype(jnp.float32) / L)[:, None]
+    count = order_table.shape[0]
+    block = 64
+    columns = far_cos.shape[1]
+    near = pl.BlockSpec((block, LANES), lambda i: (i, 0))
+    far = pl.BlockSpec((block, columns), lambda i: (i, 0))
+    return pl.pallas_call(
+        table_kernel,
+        grid=(count // block,),
+        out_shape=jax.ShapeDtypeStruct((2, count, 2 * NPHI), jnp.bfloat16),
+        in_specs=[near, near, far, far, pl.BlockSpec((block, 1), lambda i: (i, 0))],
+        out_specs=pl.BlockSpec((2, block, 2 * NPHI), lambda i: (0, i, 0)),
+        name="tables",
+    )(near_cos, near_sin, far_cos, far_sin, slopes)
+
+
+def table_kernel(near_cos_ref, near_sin_ref, far_cos_ref, far_sin_ref, slope_ref, out_ref):
+    near_cos = near_cos_ref[...]
+    near_sin = near_sin_ref[...]
+    slope = slope_ref[...]
+    for a in range(far_cos_ref.shape[1]):
+        far_cos = far_cos_ref[:, a : a + 1]
+        far_sin = far_sin_ref[:, a : a + 1]
+        cosine = far_cos * near_cos - far_sin * near_sin
+        sine = far_sin * near_cos + far_cos * near_sin
+        value = slice(a * LANES, (a + 1) * LANES)
+        turned = slice(NPHI + a * LANES, NPHI + (a + 1) * LANES)
+        out_ref[0, :, value] = cosine.astype(jnp.bfloat16)
+        out_ref[1, :, value] = (-sine).astype(jnp.bfloat16)
+        out_ref[0, :, turned] = (-sine * slope).astype(jnp.bfloat16)
+        out_ref[1, :, turned] = (-cosine * slope).astype(jnp.bfloat16)
 
 
 def latitude_kernel(rad_count, ma_count, chunks, mask_ref, radial_ref, spectrum_ref, legendre_ref, out_ref,
-                    spectrum_buf, legendre_buf, own, out_up, out_down, in_up, in_down, ready, arrived,
+                    spectrum_buf, legendre_buf, own, out_up, out_down, in_up, in_down, finished, ready, arrived,
                     fetch_sem, up_send, up_recv, down_send, down_recv, ma_send, ma_recv):
     r = lax.axis_index("rad")
     m = lax.axis_index("ma")
@@ -51,7 +74,7 @@
     _, _, slots, degrees, modes = spectrum_buf.shape
     rows = radial_ref.shape[1]
     lanes = own.shape[3]
-    share = out_ref.shape[2]
+    share = out_ref.shape[0]
 
     def fetch(c, slot):
         piece = pl.ds(c * slots, slots)
@@ -98,13 +121,21 @@
             device_id_type=MESH,
         )
 
-    def hand_over(c, d):
+    half_chunks = chunks // HALVES
+    kept_slots = half_chunks * slots
+    width = rows * kept_slots
+
+    def landing(source, h):
+        start = (source * HALVES + h) * width
+        return arrived.at[:, pl.ds(pl.multiple_of(start, width), width)]
+
+    def hand_over(h, d):
         peer = lax.rem(m + d, ma_count)
         return pltpu.make_async_remote_copy(
-            src_ref=ready.at[c, pl.ds(pl.multiple_of(peer * share, share), share)],
-            dst_ref=arrived.at[m, c],
-            send_sem=ma_send.at[c, d - 1],
-            recv_sem=ma_recv.at[c, d - 1],
+            src_ref=ready.at[h, pl.ds(pl.multiple_of(peer * share, share), share)],
+            dst_ref=landing(m, h),
+            send_sem=ma_send.at[h, d - 1],
+            recv_sem=ma_recv.at[h, d - 1],
             device_id={"ma": peer},
             device_id_type=MESH,
         )
@@ -153,10 +184,11 @@
 
     lax.fori_loop(0, chunks, compute, 0)
 
-    def relay(c):
+    def relay_up(step, here):
+        c = step - (r - 1)
         for target in range(last, 0, -1):
 
-            @pl.when((r > 0) & (r < target))
+            @pl.when(here & (r > 0) & (r < target) & (c >= 0) & (c < chunks))
             def _():
                 up(c, target).wait_recv()
                 out_up[c, target] = (
@@ -164,9 +196,11 @@
                 ).astype(jnp.bfloat16)
                 up(c, target).start()
 
+    def relay_down(step, here):
+        c = step - (last - r - 1)
         for target in range(last):
 
-            @pl.when((r < last) & (r > target))
+            @pl.when(here & (r < last) & (r > target) & (c >= 0) & (c < chunks))
             def _():
                 down(c, target).wait_recv()
                 out_down[c, target] = (
@@ -185,35 +219,52 @@
             down(c, r).wait_recv()
             own[c, r] += in_down[c, r].astype(jnp.float32)
 
-        ready[c] = own[c, r].T.astype(jnp.bfloat16)
-        for d in range(1, ma_count):
-            hand_over(c, d).start()
-        arrived[m, c] = ready[c, pl.ds(pl.multiple_of(m * share, share), share), :]
-
-    def pass_on(c, carry):
-        relay(c)
-
-        @pl.when(c > 0)
-        def _():
-            finish(c - 1)
+        first = lax.rem(c, half_chunks) * slots
+        for s in range(slots):
+            finished[pl.ds(first + s, rows, stride=kept_slots), :] = own[
+                c, r, s * rows : (s + 1) * rows, :
+            ]
+
+        @pl.when(lax.rem(c, half_chunks) == half_chunks - 1)
+        def _():
+            h = c // half_chunks
+            ready[h] = finished[...].T.astype(jnp.bfloat16)
+            for d in range(1, ma_count):
+                hand_over(h, d).start()
+            place = pl.ds(pl.multiple_of((m * HALVES + h) * width, width), width)
+            arrived[:, place] = ready[h, pl.ds(pl.multiple_of(m * share, share), share), :]
+
+    nearer_top = 2 * r > last
+    nearer_bottom = 2 * r <= last
+
+    def pass_on(step, carry):
+        relay_up(step, nearer_top)
+        relay_down(step, nearer_bottom)
+        relay_up(step, nearer_bottom)
+        relay_down(step, nearer_top)
+
+        @pl.when(step >= last - 1)
+        def _():
+            finish(step - (last - 1))
 
         return carry
 
-    lax.fori_loop(0, chunks, pass_on, 0)
-    finish(chunks - 1)
-
-    def drain(c, carry):
+    lax.fori_loop(0, chunks + last - 1, pass_on, 0)
+
+    for h in range(HALVES):
         for d in range(1, ma_count):
             sender = lax.rem(m + ma_count - d, ma_count)
             pltpu.make_async_remote_copy(
-                src_ref=ready.at[c, pl.ds(0, share)],
-                dst_ref=arrived.at[sender, c],
-                send_sem=ma_send.at[c, d - 1],
-                recv_sem=ma_recv.at[c, d - 1],
+                src_ref=ready.at[h, pl.ds(0, share)],
+                dst_ref=landing(sender, h),
+                send_sem=ma_send.at[h, d - 1],
+                recv_sem=ma_recv.at[h, d - 1],
                 device_id={"ma": sender},
                 device_id_type=MESH,
             ).wait_recv()
-            hand_over(c, d).wait_send()
+            hand_over(h, d).wait_send()
+
+    def drain(c, carry):
         for target in range(rad_count):
 
             @pl.when(r < target)
@@ -248,7 +299,7 @@
     travelling = pltpu.VMEM((chunks, rad_count, slots * rows, lanes), jnp.bfloat16)
     return pl.pallas_call(
         functools.partial(latitude_kernel, rad_count, ma_count, chunks),
-        out_shape=jax.ShapeDtypeStruct((ma_count, chunks, share, slots * rows), jnp.bfloat16),
+        out_shape=jax.ShapeDtypeStruct((share, ma_count * rows * slot_count), jnp.bfloat16),
         in_specs=[vmem, vmem, hbm, hbm],
         out_specs=vmem,
         scratch_shapes=[
@@ -259,15 +310,16 @@
             travelling,
             travelling,
             travelling,
-            pltpu.VMEM((chunks, lanes, slots * rows), jnp.bfloat16),
-            pltpu.VMEM((ma_count, chunks, share, slots * rows), jnp.bfloat16),
+            pltpu.VMEM((rows * slot_count // HALVES, lanes), jnp.float32),
+            pltpu.VMEM((HALVES, lanes, rows * slot_count // HALVES), jnp.bfloat16),
+            pltpu.VMEM((share, ma_count * rows * slot_count), jnp.bfloat16),
             dma((2, 2)),
             dma((chunks, rad_count)),
             dma((chunks, rad_count)),
             dma((chunks, rad_count)),
             dma((chunks, rad_count)),
-            dma((chunks, ma_count - 1)),
-            dma((chunks, ma_count - 1)),
+            dma((HALVES, ma_count - 1)),
+            dma((HALVES, ma_count - 1)),
         ],
         compiler_params=pltpu.CompilerParams(
             collective_id=1, has_side_effects=True, vmem_limit_bytes=56 * 1024 * 1024
@@ -417,16 +469,16 @@
     if (
         latitude_count % (rad_count * LANES) == 0
         and degree_count % LANES == 0
-        and slot_count % GROUP == 0
-        and GROUP * level_count * 4 % LANES == 0
+        and slot_count % (GROUP * HALVES) == 0
+        and slot_count // HALVES * level_count * 4 % LANES == 0
+        and rad_count > 2
         and lat_rows % 16 == 0
     ):
         received = latitude_exchange(spectrum, radial_table, legendre, allowed, GROUP)
+        groups = ma_count * HALVES
         coefficients = received.reshape(
-            ma_count, slot_count // GROUP, lat_rows, GROUP, level_count, 2, 2
-        )
-        coefficients = coefficients.transpose(2, 4, 5, 6, 0, 1, 3)
-        coefficients = coefficients.reshape(lat_rows, level_count, 2, 2, ma_count * slot_count)
+            lat_rows, groups, level_count, 2, 2, slot_count // HALVES
+        )
     else:
         masked_table = jnp.where(allowed[:, :, None], legendre, jnp.zeros_like(legendre))
         levels = jnp.einsum(
@@ -442,10 +494,10 @@
         latitudes = jnp.sum(pieces.astype(jnp.float32), axis=0).astype(jnp.bfloat16)
         received = lax.all_to_all(latitudes, "ma", split_axis=0, concat_axis=1, tiled=True)
         coefficients = received.reshape(lat_rows, ma_count, level_count, 2, 2, slot_count)
-        coefficients = coefficients.transpose(0, 2, 3, 4, 1, 5)
-        coefficients = coefficients.reshape(lat_rows, level_count, 2, 2, ma_count * slot_count)
+        groups = ma_count
+    tables = tables.reshape(2, groups, ma_count * slot_count // groups, 2 * NPHI)
     synthesis = jnp.einsum(
-        "trfik,ikq->ftrq", coefficients, tables, preferred_element_type=jnp.float32
+        "tsrfik,iskq->ftrq", coefficients, tables, preferred_element_type=jnp.float32
     ).astype(jnp.bfloat16)
     fields = synthesis[..., :NPHI].astype(jnp.float32)
     slope_field = synthesis[..., NPHI:].astype(jnp.float32)

time: 171 us -> 142 us (0.83)
  local copies, waits for them, and re-layouts: 35.8 us -> 14.6 us
  Pallas kernels: 116 us -> 104 us
  matrix products: 9.06 us -> 13.9 us
  other arithmetic: 9.2 us -> 7.35 us
    pallas_call x1, Pallas kernels: 90.5 us -> 71.8 us  [latitude_exchange(): pl.pallas_call(functools.partial(latitude_kernel, rad_count, ma_count, ch...]
    transpose x1 -> x0, local copies, waits for them, and re-layouts: 12.7 us -> none  [on_device(): coefficients = coefficients.transpose(2, 4, 5, 6, 0, 1, 3)]
    convert_element_type x1, local copies, waits for them, and re-layouts: 7.31 us -> 0.12 us  [turn(): angles = phase_index.astype(jnp.float32) * (2.0 * math.pi / NPHI)]
    pallas_call x1 -> x0, local copies, waits for them, and re-layouts: 6.38 us -> none  [latitude_exchange(): pl.pallas_call(functools.partial(latitude_kernel, rad_count, ma_count, ch...]
    pallas_call x0 -> x1, Pallas kernels: none -> 6.33 us  [synthesis_tables(): pl.pallas_call(table_kernel, grid=(count // block,), out_shape=jax.ShapeD...]
    dot_general x1, matrix products: 6.25 us -> 11.1 us  [on_device(): jnp.einsum('tsrfik,iskq->ftrq', coefficients, tables, preferred_element_t...]
    reshape x0 -> x1, local copies, waits for them, and re-layouts: none -> 4.46 us  [on_device(): received.reshape(lat_rows, groups, level_count, 2, 2, slot_count // HALVES)]
    concatenate x1 -> x0, other arithmetic: 2.44 us -> none  [synthesis_tables(): tables = jnp.concatenate([values, turned], axis=2).astype(jnp.bfloat16)]
where the time goes in v3:
time: 142 us; the launch traced here: 141 us
  Pallas kernels  104 us (73%)
  local copies, waits for them, and re-layouts  14.6 us (10%)
  matrix products  13.9 us (10%)
  other arithmetic  7.35 us (5%)
    pallas_call x1, Pallas kernels, latitude_exchange(): pl.pallas_call(functools.partial(latitude_kernel, rad_count, ma_count, ch...  71.8 us
    pallas_call x1, Pallas kernels, column_exchange(): pl.pallas_call(functools.partial(column_kernel, rad_count, ma_count), out...  25.9 us
    dot_general x1, matrix products, on_device(): jnp.einsum('tsrfik,iskq->ftrq', coefficients, tables, preferred_element_t...  11.1 us
    pallas_call x1, Pallas kernels, synthesis_tables(): pl.pallas_call(table_kernel, grid=(count // block,), out_shape=jax.ShapeD...  6.33 us
    reshape x1, local copies, waits for them, and re-layouts, on_device(): received.reshape(lat_rows, groups, level_count, 2, 2, slot_count // HALVES)  4.46 us

profile of v3, /device:TPU:1, one launch (start us, length us, event | category | flops | bytes accessed | tf_op | source)
XLA Modules:
  0.0 140.6 jit_solution(2391669939461023355)
XLA Ops:
  0.6 0.8 dynamic_slice.6
  1.4 0.7 compare_convert_fusion.mask_ref
  2.1 0.8 multiply_bitcast_fusion
  3.0 0.7 reshape.84.radial_ref
  3.7 71.8 %latitude_exchange.1 = bf16[16,24576]{1,0:T(8,128)(2,1)} custom-call(f32[64,1,128]{2,1,0:T(1,128)} %compare_convert_fusion.mask_ref, bf16[4,48,384]{2,1,0:T(8,128)(2,1)} %reshape.84.radial_ref, bf16[4,64,128,384]{3,2,1,0:T(8,128)(2,1)} %spectrum_ref.1, bf16[64,128,512]{2,1,0:T(8,128)(2,1)} %legendre_ref.1), custom_call_target="tpu_custom_call" | custom-call | tf_op jit(solution)/shard_map/latitude_exchange/pallas_call | solution.py:300
  75.5 0.0 copy-start.1
  75.5 4.5 %reshape.85 = bf16[16,16,12,2,2,32]{5,4,3,2,1,0:T(2,128)(2,1)} reshape(bf16[16,24576]{1,0:T(8,128)(2,1)} %latitude_exchange.1) | data formatting | bytes 1572864 | tf_op jit(solution)/shard_map/reshape | solution.py:479
  80.0 0.0 copy-done.1
  80.0 0.1 fusion.23
  80.1 0.1 copy.20
  80.2 1.9 %sine_multiply_fusion = (f32[512,8]{1,0:T(8,128)}, f32[512,8]{1,0:T(8,128)}) fusion(f32[512,8]{1,0:T(8,128)S(1)} %copy.20, f32[512]{0:T(512)S(1)} %get-tuple-element.17), kind=kLoop, calls=%fused_computation.18 | loop fusion | flops 12288 | bytes 51200 | tf_op jit(solution)/shard_map/mul | solution.py:34
  82.1 1.9 %fusion.17 = (f32[512,128]{1,0:T(8,128)}, f32[512,128]{1,0:T(8,128)}) fusion(s32[512]{0:T(512)S(1)} %copy-done.1), kind=kLoop, calls=%fused_computation.24 | loop fusion | flops 917504 | bytes 526336 | tf_op jit(solution)/shard_map/sin | solution.py:28
  84.0 0.9 copy.21.slope_ref
  84.9 6.3 %tables.1 = bf16[2,512,2048]{2,1,0:T(8,128)(2,1)} custom-call(f32[512,128]{1,0:T(8,128)} %get-tuple-element.19.near_cos_ref, f32[512,128]{1,0:T(8,128)} %get-tuple-element.18.near_sin_ref, f32[512,8]{1,0:T(8,128)} %get-tuple-element.15.far_cos_ref, f32[512,8]{1,0:T(8,128)} %get-tuple-element.14.far_sin_ref, f32[512,1]{1,0:T(8,128)} %copy.21.slope_ref), custom_call_target="tpu_custom_call" | custom-call | tf_op jit(solution)/shard_map/tables/pallas_call | solution.py:41
  91.2 11.1 %fusion.4 = bf16[2,16,12,2048]{3,1,0,2:T(8,128)(2,1)S(1)} fusion(bf16[2,16,32,2048,1,1]{3,2,1,0,5,4:T(8,128)(2,1)} %bitcast.24, bf16[16,16,12,2,2,32]{5,4,3,2,1,0:T(2,128)(2,1)} %reshape.85), kind=kOutput, calls=%fused_computation.3 | convolution fusion | flops 1611399168 | bytes 6553600 | tf_op jit(solution)/shard_map/tsrfik,iskq->ftrq/dot_general | solution.py:499
  102.3 0.2 slice_convert_fusion
  102.5 0.1 fusion.7
  102.6 0.0 copy-start
  102.6 0.0 copy-start.2
  102.6 0.5 copy.24
  103.1 0.1 sub.11
  103.2 0.1 copy-done
  103.3 0.1 eq.42
  103.4 0.0 copy-done.2
  103.4 0.1 mul.124
  103.5 1.4 fusion.8.partial_ref
  104.8 25.9 %column_exchange.1 = (f32[16,1024]{1,0:T(8,128)}, bf16[2,128,1024]{2,1,0:T(8,128)(2,1)}) custom-call(f32[128,1024]{1,0:T(8,128)} %fusion.8.partial_ref), custom_call_target="tpu_custom_call" | custom-call | tf_op jit(solution)/shard_map/column_exchange/pallas_call | solution.py:428
  130.7 1.4 %convolution_bitcast_fusion = f32[2,192,1024]{2,1,0:T(8,128)S(1)} fusion(bf16[2,128,1024]{2,1,0:T(8,128)(2,1)} %get-tuple-element.5, s32[192]{0:T(256)S(1)} %eq.42), kind=kOutput, calls=%fused_computation.5 | convolution fusion | flops 100687872 | bytes 2097920 | tf_op jit(solution)/shard_map/pj,cjq->cpq/dot_general | solution.py:514
  132.2 1.0 fusion.26
  133.2 0.1 mul.149
  133.3 0.5 copy.26
  133.7 1.2 mul.152
  135.0 1.3 copy.27
  136.3 0.1 copy.25
  136.4 1.6 %multiply_subtract_fusion = f32[2,16,12,1024]{3,1,0,2:T(8,128)S(1)} fusion(bf16[2,16,12,2048]{3,1,0,2:T(8,128)(2,1)S(1)} %fusion.4, f32[16,12,1024]{2,0,1:T(8,128)} %copy.27, f32[16,12,1024]{2,0,1:T(8,128)S(1)} %copy.26, f32[16,12]{0,1:T(8,128)S(1)} %copy.25), kind=kLoop, calls=%fused_computation.4 | loop fusion | flops 2752512 | bytes 4719360 | tf_op jit(solution)/shard_map/sub | solution.py:517
  138.0 1.2 copy.28
  139.3 1.3 constant_dynamic-slice_fusion
  (6 shorter events, 0.0 us)
Async XLA Ops:
  75.5 4.5 %copy-start.1 = (s32[512]{0:T(512)S(1)}, s32[512]{0:T(512)}, u32[]{:S(2)}) copy-start(s32[512]{0:T(512)} %param.9) | copy-start | bytes 6148
  102.6 0.7 copy-start
  102.6 0.8 copy-start.2

commit v4 on v3

--- a/solution.py
+++ b/solution.py
@@ -13,7 +13,7 @@
 QROWS = 16
 LANES = 128
 GROUP = 8
-HALVES = 2
+HALVES = 1
 MESH = pl.DeviceIdType.MESH
 
 
@@ -33,39 +33,42 @@
     far_cos = far_cos * weights[:, None]
     far_sin = far_sin * weights[:, None]
     slopes = (order_table.astype(jnp.float32) / L)[:, None]
-    count = order_table.shape[0]
-    block = 64
-    columns = far_cos.shape[1]
-    near = pl.BlockSpec((block, LANES), lambda i: (i, 0))
-    far = pl.BlockSpec((block, columns), lambda i: (i, 0))
+    return near_cos, near_sin, far_cos, far_sin, slopes
+
+
+def plain_tables(pieces):
+    count = pieces[0].shape[0]
+    whole = pl.BlockSpec(memory_space=pltpu.VMEM)
     return pl.pallas_call(
-        table_kernel,
-        grid=(count // block,),
+        functools.partial(write_tables, slice(None)),
         out_shape=jax.ShapeDtypeStruct((2, count, 2 * NPHI), jnp.bfloat16),
-        in_specs=[near, near, far, far, pl.BlockSpec((block, 1), lambda i: (i, 0))],
-        out_specs=pl.BlockSpec((2, block, 2 * NPHI), lambda i: (0, i, 0)),
+        in_specs=[whole] * 5,
+        out_specs=whole,
         name="tables",
-    )(near_cos, near_sin, far_cos, far_sin, slopes)
-
-
-def table_kernel(near_cos_ref, near_sin_ref, far_cos_ref, far_sin_ref, slope_ref, out_ref):
-    near_cos = near_cos_ref[...]
-    near_sin = near_sin_ref[...]
-    slope = slope_ref[...]
+    )(*pieces)
+
+
+def write_tables(block, near_cos_ref, near_sin_ref, far_cos_ref, far_sin_ref, slope_ref, out_ref):
+    near_cos = near_cos_ref[block, :]
+    near_sin = near_sin_ref[block, :]
+    slope = slope_ref[block, :]
+    far_cos_all = far_cos_ref[block, :]
+    far_sin_all = far_sin_ref[block, :]
     for a in range(far_cos_ref.shape[1]):
-        far_cos = far_cos_ref[:, a : a + 1]
-        far_sin = far_sin_ref[:, a : a + 1]
+        far_cos = far_cos_all[:, a : a + 1]
+        far_sin = far_sin_all[:, a : a + 1]
         cosine = far_cos * near_cos - far_sin * near_sin
         sine = far_sin * near_cos + far_cos * near_sin
         value = slice(a * LANES, (a + 1) * LANES)
         turned = slice(NPHI + a * LANES, NPHI + (a + 1) * LANES)
-        out_ref[0, :, value] = cosine.astype(jnp.bfloat16)
-        out_ref[1, :, value] = (-sine).astype(jnp.bfloat16)
-        out_ref[0, :, turned] = (-sine * slope).astype(jnp.bfloat16)
-        out_ref[1, :, turned] = (-cosine * slope).astype(jnp.bfloat16)
-
-
-def latitude_kernel(rad_count, ma_count, chunks, mask_ref, radial_ref, spectrum_ref, legendre_ref, out_ref,
+        out_ref[0, block, value] = cosine.astype(jnp.bfloat16)
+        out_ref[1, block, value] = (-sine).astype(jnp.bfloat16)
+        out_ref[0, block, turned] = (-sine * slope).astype(jnp.bfloat16)
+        out_ref[1, block, turned] = (-cosine * slope).astype(jnp.bfloat16)
+
+
+def latitude_kernel(rad_count, ma_count, chunks, mask_ref, radial_ref, near_cos_ref, near_sin_ref,
+                    far_cos_ref, far_sin_ref, slope_ref, spectrum_ref, legendre_ref, out_ref, table_ref,
                     spectrum_buf, legendre_buf, own, out_up, out_down, in_up, in_down, finished, ready, arrived,
                     fetch_sem, up_send, up_recv, down_send, down_recv, ma_send, ma_recv):
     r = lax.axis_index("rad")
@@ -237,6 +240,8 @@
     nearer_top = 2 * r > last
     nearer_bottom = 2 * r <= last
 
+    table_block = table_ref.shape[1] // chunks
+
     def pass_on(step, carry):
         relay_up(step, nearer_top)
         relay_down(step, nearer_bottom)
@@ -246,6 +251,13 @@
         @pl.when(step >= last - 1)
         def _():
             finish(step - (last - 1))
+
+        @pl.when(step < chunks)
+        def _():
+            write_tables(
+                pl.ds(pl.multiple_of(step * table_block, table_block), table_block),
+                near_cos_ref, near_sin_ref, far_cos_ref, far_sin_ref, slope_ref, table_ref,
+            )
 
         return carry
 
@@ -281,7 +293,7 @@
     out_ref[...] = arrived[...]
 
 
-def latitude_exchange(spectrum, radial_table, legendre, allowed, slots):
+def latitude_exchange(spectrum, radial_table, legendre, allowed, pieces, slots):
     rad_count = lax.axis_size("rad")
     ma_count = lax.axis_size("ma")
     parts, slot_count, degrees, modes = spectrum.shape
@@ -299,9 +311,12 @@
     travelling = pltpu.VMEM((chunks, rad_count, slots * rows, lanes), jnp.bfloat16)
     return pl.pallas_call(
         functools.partial(latitude_kernel, rad_count, ma_count, chunks),
-        out_shape=jax.ShapeDtypeStruct((share, ma_count * rows * slot_count), jnp.bfloat16),
-        in_specs=[vmem, vmem, hbm, hbm],
-        out_specs=vmem,
+        out_shape=(
+            jax.ShapeDtypeStruct((share, ma_count * rows * slot_count), jnp.bfloat16),
+            jax.ShapeDtypeStruct((2, ma_count * slot_count, 2 * NPHI), jnp.bfloat16),
+        ),
+        in_specs=[vmem] * 7 + [hbm, hbm],
+        out_specs=(vmem, vmem),
         scratch_shapes=[
             pltpu.VMEM((2, parts, slots, degrees, modes), jnp.bfloat16),
             pltpu.VMEM((2, slots, degrees, latitude_count), jnp.bfloat16),
@@ -325,7 +340,7 @@
             collective_id=1, has_side_effects=True, vmem_limit_bytes=56 * 1024 * 1024
         ),
         name="latitude_exchange",
-    )(allowed.astype(jnp.float32)[:, None, :], spread, spectrum, legendre)
+    )(allowed.astype(jnp.float32)[:, None, :], spread, *pieces, spectrum, legendre)
 
 
 def column_kernel(rad_count, ma_count, partial_ref, sum_ref, velocity_ref, arrived, mine, beside, whole,
@@ -464,7 +479,7 @@
     my_orders = lax.dynamic_slice_in_dim(order_table, lax.axis_index("ma") * slot_count, slot_count)
     my_degrees = lax.axis_index("rad") * degree_count + jnp.arange(degree_count, dtype=jnp.int32)
     allowed = my_degrees[None, :] >= my_orders[:, None]
-    tables = synthesis_tables(order_table)
+    pieces = synthesis_tables(order_table)
     lat_rows = latitude_count // (rad_count * ma_count)
     if (
         latitude_count % (rad_count * LANES) == 0
@@ -474,12 +489,15 @@
         and rad_count > 2
         and lat_rows % 16 == 0
     ):
-        received = latitude_exchange(spectrum, radial_table, legendre, allowed, GROUP)
+        received, tables = latitude_exchange(
+            spectrum, radial_table, legendre, allowed, pieces, GROUP
+        )
         groups = ma_count * HALVES
         coefficients = received.reshape(
             lat_rows, groups, level_count, 2, 2, slot_count // HALVES
         )
     else:
+        tables = plain_tables(pieces)
         masked_table = jnp.where(allowed[:, :, None], legendre, jnp.zeros_like(legendre))
         levels = jnp.einsum(
             "rn,ckln->rckl", radial_table, spectrum, preferred_element_type=jnp.float32
@@ -487,11 +505,11 @@
         contribution = jnp.einsum(
             "klt,rckl->trck", masked_table, levels, preferred_element_type=jnp.float32
         )
-        pieces = contribution.astype(jnp.bfloat16).reshape(
+        sums = contribution.astype(jnp.bfloat16).reshape(
             rad_count, latitude_count // rad_count, level_count * 4 * slot_count
         )
-        pieces = lax.all_to_all(pieces, "rad", split_axis=0, concat_axis=0, tiled=True)
-        latitudes = jnp.sum(pieces.astype(jnp.float32), axis=0).astype(jnp.bfloat16)
+        sums = lax.all_to_all(sums, "rad", split_axis=0, concat_axis=0, tiled=True)
+        latitudes = jnp.sum(sums.astype(jnp.float32), axis=0).astype(jnp.bfloat16)
         received = lax.all_to_all(latitudes, "ma", split_axis=0, concat_axis=1, tiled=True)
         coefficients = received.reshape(lat_rows, ma_count, level_count, 2, 2, slot_count)
         groups = ma_count

time: 142 us -> 133 us (0.937)
  matrix products: 13.9 us -> 8.89 us
  Pallas kernels: 104 us -> 101 us
  local copies, waits for them, and re-layouts: 14.6 us -> 12.5 us
  other arithmetic: 7.35 us -> 8.84 us
    pallas_call x1 -> x0, Pallas kernels: 6.33 us -> none  [synthesis_tables(): pl.pallas_call(table_kernel, grid=(count // block,), out_shape=jax.ShapeD...]
    dot_general x1, matrix products: 11.1 us -> 6.07 us  [on_device(): jnp.einsum('tsrfik,iskq->ftrq', coefficients, tables, preferred_element_t...]
    pallas_call x1, Pallas kernels: 71.8 us -> 75.7 us  [latitude_exchange(): pl.pallas_call(functools.partial(latitude_kernel, rad_count, ma_count, ch...]
    reshape x1, local copies, waits for them, and re-layouts: 4.46 us -> 2.51 us  [on_device(): received.reshape(lat_rows, groups, level_count, 2, 2, slot_count // HALVES)]
where the time goes in v4:
time: 133 us; the launch traced here: 132 us
  Pallas kernels  101 us (76%)
  local copies, waits for them, and re-layouts  12.5 us (9%)
  matrix products  8.89 us (7%)
  other arithmetic  8.84 us (7%)
    pallas_call x1, Pallas kernels, latitude_exchange(): pl.pallas_call(functools.partial(latitude_kernel, rad_count, ma_count, ch...  75.7 us
    pallas_call x1, Pallas kernels, column_exchange(): pl.pallas_call(functools.partial(column_kernel, rad_count, ma_count), out...  25.5 us
    dot_general x1, matrix products, on_device(): jnp.einsum('tsrfik,iskq->ftrq', coefficients, tables, preferred_element_t...  6.07 us

profile of v4, /device:TPU:1, one launch (start us, length us, event | category | flops | bytes accessed | tf_op | source)
XLA Modules:
  0.0 132.2 jit_solution(827822072057337652)
XLA Ops:
  0.6 0.0 copy-start.1
  0.6 0.8 dynamic_slice.6
  1.4 0.7 compare_convert_fusion.mask_ref
  2.2 0.8 convert_multiply_fusion
  2.9 0.8 fusion.18
  3.7 0.1 copy.21
  3.8 1.9 %sine_multiply_fusion = (f32[512,8]{1,0:T(8,128)}, f32[512,8]{1,0:T(8,128)}) fusion(f32[512,8]{1,0:T(8,128)S(1)} %copy.21, f32[512]{0:T(512)S(1)} %get-tuple-element.21), kind=kLoop, calls=%fused_computation.17 | loop fusion | flops 12288 | bytes 51200 | tf_op jit(solution)/shard_map/mul | solution.py:34
  5.7 2.6 %fusion.12 = (f32[512,128]{1,0:T(8,128)}, f32[512,128]{1,0:T(8,128)}) fusion(s32[512]{0:T(512)} %param.9), kind=kLoop, calls=%fused_computation.23 | loop fusion | flops 917504 | bytes 526336 | tf_op jit(solution)/shard_map/sin | solution.py:28
  8.3 0.8 copy.22.slope_ref
  9.2 0.0 copy-done.1
  9.2 0.1 multiply_bitcast_fusion
  9.3 0.7 reshape.83.radial_ref
  10.0 75.7 %latitude_exchange.1 = (bf16[16,24576]{1,0:T(8,128)(2,1)}, bf16[2,512,2048]{2,1,0:T(8,128)(2,1)}) custom-call(f32[64,1,128]{2,1,0:T(1,128)} %compare_convert_fusion.mask_ref, bf16[4,48,384]{2,1,0:T(8,128)(2,1)} %reshape.83.radial_ref, f32[512,128]{1,0:T(8,128)} %get-tuple-element.23.near_cos_ref, f32[512,128]{1,0:T(8,128)} %get-tuple-element.22.near_sin_ref, ...), custom_call_target="tpu_custom_call" | custom-call | tf_op jit(solution)/shard_map/latitude_exchange/pallas_call | solution.py:312
  85.7 2.5 %reshape.85 = bf16[16,8,12,2,2,64]{5,4,3,2,1,0:T(2,128)(2,1)S(1)} reshape(bf16[16,24576]{1,0:T(8,128)(2,1)} %get-tuple-element.7) | data formatting | bytes 1572864 | tf_op jit(solution)/shard_map/reshape | solution.py:496
  88.3 6.1 %fusion = bf16[2,16,12,2048]{3,1,0,2:T(8,128)(2,1)S(1)} fusion(bf16[2,8,64,2048,1,1]{3,2,1,0,5,4:T(8,128)(2,1)} %bitcast.26, bf16[16,8,12,2,2,64]{5,4,3,2,1,0:T(2,128)(2,1)S(1)} %reshape.85), kind=kOutput, calls=%fused_computation.1 | convolution fusion | flops 1611399168 | bytes 6553600 | tf_op jit(solution)/shard_map/tsrfik,iskq->ftrq/dot_general | solution.py:517
  94.3 0.2 slice_convert_fusion
  94.5 0.1 fusion.2
  94.6 0.0 copy-start
  94.6 0.0 copy-start.2
  94.6 0.5 copy.24
  95.1 0.1 sub.11
  95.2 0.1 copy-done
  95.3 0.1 eq.42
  95.4 0.0 copy-done.2
  95.4 0.1 mul.124
  95.5 1.4 %fusion.3.partial_ref = f32[128,1024]{1,0:T(8,128)} fusion(f32[192,1024]{1,0:T(8,128)S(1)} %sub.11, f32[192]{0:T(256)S(1)} %mul.124, s32[192]{0:T(256)S(1)} %eq.42), kind=kOutput, calls=%fused_computation.8 | convolution fusion | flops 302211072 | bytes 1312256 | tf_op jit(solution)/shard_map/dot_general | solution.py:527
  96.9 25.5 %column_exchange.1 = (f32[16,1024]{1,0:T(8,128)}, bf16[2,128,1024]{2,1,0:T(8,128)(2,1)}) custom-call(f32[128,1024]{1,0:T(8,128)} %fusion.3.partial_ref), custom_call_target="tpu_custom_call" | custom-call | tf_op jit(solution)/shard_map/column_exchange/pallas_call | solution.py:443
  122.4 1.4 %convolution_bitcast_fusion = f32[2,192,1024]{2,1,0:T(8,128)S(1)} fusion(bf16[2,128,1024]{2,1,0:T(8,128)(2,1)} %get-tuple-element.9, s32[192]{0:T(256)S(1)} %eq.42), kind=kOutput, calls=%fused_computation.4 | convolution fusion | flops 100687872 | bytes 2097920 | tf_op jit(solution)/shard_map/pj,cjq->cpq/dot_general | solution.py:532
  123.8 1.0 fusion.21
  124.8 0.1 mul.149
  124.9 0.5 copy.26
  125.4 1.2 mul.152
  126.6 1.3 %copy.27 = f32[16,12,1024]{2,0,1:T(8,128)} copy(f32[16,12,1024]{2,1,0:T(8,128)S(1)} %mul.152) | data formatting | bytes 1572864 | tf_op jit(solution)/shard_map/mul | solution.py:536
  127.9 0.1 copy.25
  128.0 1.7 %multiply_subtract_fusion = f32[2,16,12,1024]{3,1,0,2:T(8,128)S(1)} fusion(bf16[2,16,12,2048]{3,1,0,2:T(8,128)(2,1)S(1)} %fusion, f32[16,12,1024]{2,0,1:T(8,128)} %copy.27, f32[16,12,1024]{2,0,1:T(8,128)S(1)} %copy.26, f32[16,12]{0,1:T(8,128)S(1)} %copy.25), kind=kLoop, calls=%fused_computation.3 | loop fusion | flops 2752512 | bytes 4719360 | tf_op jit(solution)/shard_map/sub | solution.py:535
  129.7 1.2 copy.28
  130.9 1.3 %constant_dynamic-slice_fusion = f32[16,256]{1,0:T(8,128)} fusion(f32[16,1024]{1,0:T(8,128)} %get-tuple-element.8, s32[]{:T(128)S(6)} %select_n.27), kind=kLoop, calls=%fused_computation.45 | loop fusion | bytes 32772 | tf_op jit(solution)/shard_map/dynamic_slice | solution.py:467
  (5 shorter events, 0.0 us)
Async XLA Ops:
  0.6 8.6 %copy-start.1 = (bf16[12,384]{1,0:T(8,128)(2,1)S(1)}, bf16[12,384]{1,0:T(8,128)(2,1)}, u32[]{:S(2)}) copy-start(bf16[12,384]{1,0:T(8,128)(2,1)} %param.7) | copy-start | bytes 27652
  94.6 0.7 copy-start
  94.6 0.8 copy-start.2
